TPU v7x, 32 devices: a whole 2x2x4 slice. The times are simulated.
32 devices in a mesh: grp: 2 (over x), seq: 16 (over z, y, core).
Axes of the slice: x: 2, y: 2, z: 4, core: 2. Of those that a mesh axis runs over, the one named last changes fastest.
Arguments:
- queries: bfloat16 [16384, 1536], P(('grp', 'seq')), parts along dimension 0, may hold values from -26 to 26
- keys_values: bfloat16 [2, 16384, 1536], P(None, ('grp', 'seq')), parts along dimension 1, may hold values from -26 to 26
- segment_ids: int32 [16384], P('grp'), parts along dimension 0, may hold values from 0 to 31, never falling along the last dimension, each value on 1 to 512 neighbouring positions
- route_shard: int32 [16384, 1], P(('grp', 'seq')), parts along dimension 0, may hold values from 0 to 15; in each aligned block of 512 rows (0 to 511, 512 to 1023, ...) at most 64 rows name the same one
- route_slot: int32 [16384], P(('grp', 'seq')), parts along dimension 0, may hold values from 0 to 511
- control_proj: bfloat16 [1536, 3072], replicated, may hold values from -0.15625 to 0.15625
- base_hidden: bfloat16 [16384, 3072], P(('grp', 'seq')), parts along dimension 0, may hold values from -6 to 6
- cotangent: bfloat16 [16384, 3072], P(('grp', 'seq')), parts along dimension 0, may hold values from -1.25 to 1.25
Outputs:
- mixed_hidden: bfloat16 [16384, 3072], P(('grp', 'seq')), parts along dimension 0
- proj_grad: float32 [3072, 3072], P(('grp', 'seq')), parts along dimension 0
There are 2 independent parts, one for each index of `grp`. A program takes and returns all parts, laid end to end along the dimension named above; an argument that names none is the same for every part. Nothing has to cross between parts.
Inputs may be any that keep to these rules, and one draw needn't show every extreme that they name: `segment_ids`: segment numbers never fall along the sequence; each image spans 1 to 512 tokens, one exactly 512. `route_shard`: of the 512 rows of one device, at most 64 name the same base shard; in every draw some device sends exactly 64 rows to one shard.
All inputs are finite; a program needn't handle non-finite values.
Results may differ from a plain program's by a relative error of at most 0.008.
Values may be sent and summed in bfloat16 or wider, within the bound.
No kernel may reach another device: no remote copies, remote signals or barrier semaphores. Data moves between devices by JAX's collectives and lax.ppermute only.
A program may use at most 192 MiB of HBM per device.

v0:
```python
import functools
import math

import jax
import jax.numpy as jnp
from jax import lax
from jax.experimental import pallas as pl
from jax.experimental.pallas import tpu as pltpu
from jax.sharding import PartitionSpec as P

HEAD = 128
SEG_MAX = 512
QUERY_BLOCK = 128
KEY_BLOCK = 256
OUTER_PARTS = 2
INNER_PARTS = 2
LOCAL_FLOPS_HINT = 1 << 33
HALO_FLOPS_HINT = 1 << 34
MASKED = -1e30
EXP2_SCALE = HEAD ** (-0.5) * math.log2(math.e)


def attend_step(pairs, key_seg_ref, query_seg, queries, key_block, state):
    offset = pl.multiple_of(key_block * KEY_BLOCK, KEY_BLOCK)
    keep = key_seg_ref[pl.ds(offset, KEY_BLOCK), :] == query_seg
    result = []
    for (pair_ref, head), query, (peak, total, summed) in zip(pairs, queries, state):
        keys = pair_ref[0, pl.ds(offset, KEY_BLOCK), head]
        values = pair_ref[1, pl.ds(offset, KEY_BLOCK), head]
        scores = lax.dot_general(
            keys, query, (((1,), (1,)), ((), ())), preferred_element_type=jnp.float32
        )
        scores = jnp.where(keep, scores, MASKED)
        new_peak = jnp.maximum(peak, jnp.max(scores, axis=0, keepdims=True))
        weights = jnp.exp2((scores - new_peak) * EXP2_SCALE)
        shrink = jnp.exp2((peak - new_peak) * EXP2_SCALE)
        total = total * shrink + jnp.sum(weights, axis=0, keepdims=True)
        summed = summed * shrink + lax.dot_general(
            values,
            weights.astype(jnp.bfloat16),
            (((0,), (0,)), ((), ())),
            preferred_element_type=jnp.float32,
        )
        result.append((new_peak, total, summed))
    return tuple(result)


def head_slices(width):
    return [slice(start, start + HEAD) for start in range(0, width, HEAD)]


def local_kernel(
    bounds, first_query_ref, last_query_ref, first_own_ref, last_own_ref, query_seg_ref,
    key_seg_ref, summed_ref, stats_ref,
):
    block = pl.program_id(0)
    heads = head_slices(first_query_ref.shape[1])
    state = tuple(
        (
            jnp.full((1, QUERY_BLOCK), MASKED, jnp.float32),
            jnp.zeros((1, QUERY_BLOCK), jnp.float32),
            jnp.zeros((HEAD, QUERY_BLOCK), jnp.float32),
        )
        for _ in range(2 * len(heads))
    )
    state = lax.fori_loop(
        bounds[block, 2],
        bounds[block, 3],
        functools.partial(
            attend_step,
            [(ref, head) for ref in (first_own_ref, last_own_ref) for head in heads],
            key_seg_ref,
            query_seg_ref[...],
            [ref[:, head] for ref in (first_query_ref, last_query_ref) for head in heads],
        ),
        state,
    )
    for h, (peak, total, summed) in enumerate(state):
        stats_ref[0, h : h + 1, :] = peak
        stats_ref[1, h : h + 1, :] = total
        summed_ref[h * HEAD : (h + 1) * HEAD, :] = summed


def halo_kernel(
    bounds, first_query_ref, last_query_ref, before_ref, after_ref, query_seg_ref,
    before_seg_ref, after_seg_ref, summed_ref, stats_ref, place_ref, out_ref, attended_ref,
):
    block = pl.program_id(0)
    half_width = first_query_ref.shape[1]
    heads = head_slices(2 * half_width)
    queries = [
        ref[:, head] for ref in (first_query_ref, last_query_ref) for head in head_slices(half_width)
    ]
    state = tuple(
        (stats_ref[0, h : h + 1, :], stats_ref[1, h : h + 1, :], summed_ref[head, :])
        for h, head in enumerate(heads)
    )
    for column, pair_ref, seg_ref in ((0, before_ref, before_seg_ref), (4, after_ref, after_seg_ref)):
        state = lax.fori_loop(
            bounds[block, column],
            bounds[block, column + 1],
            functools.partial(
                attend_step,
                [(pair_ref, head) for head in heads],
                seg_ref,
                query_seg_ref[...],
                queries,
            ),
            state,
        )
    rows = pl.ds(pl.multiple_of(block * QUERY_BLOCK, QUERY_BLOCK), QUERY_BLOCK)
    for head, (peak, total, summed) in zip(heads, state):
        attended_ref[rows, head] = (summed * (1.0 / total)).T.astype(jnp.bfloat16)

    @pl.when(block == pl.num_programs(0) - 1)
    def _():
        out_ref[...] = jnp.dot(
            place_ref[...], attended_ref[...], preferred_element_type=jnp.float32
        ).astype(jnp.bfloat16)


def whole(*shape):
    return pl.BlockSpec(shape, lambda i, b: (0,) * len(shape))


def at_column(shape, column):
    return pl.BlockSpec(shape, lambda i, b: (0,) * (len(shape) - 1) + (column,))


def query_rows(width, column):
    return pl.BlockSpec((QUERY_BLOCK, width), lambda i, b: (i, column))


def query_lanes(*shape):
    return pl.BlockSpec(shape + (QUERY_BLOCK,), lambda i, b: (0,) * len(shape) + (i,))


def attend_local(queries, pairs, quarters, query_seg, bounds):
    row_count, width = queries.shape
    quarter = width // 4
    head_count = width // (2 * HEAD)
    return pl.pallas_call(
        local_kernel,
        out_shape=(
            jax.ShapeDtypeStruct((2 * quarter, row_count), jnp.float32),
            jax.ShapeDtypeStruct((2, head_count, row_count), jnp.float32),
        ),
        grid_spec=pltpu.PrefetchScalarGridSpec(
            num_scalar_prefetch=1,
            grid=(row_count // QUERY_BLOCK,),
            in_specs=[query_rows(quarter, q) for q in quarters]
            + [at_column((2, row_count, quarter), q) for q in quarters]
            + [query_lanes(1), whole(row_count, 1)],
            out_specs=[query_lanes(2 * quarter), query_lanes(2, head_count)],
        ),
        compiler_params=pltpu.CompilerParams(vmem_limit_bytes=48 << 20),
        cost_estimate=pl.CostEstimate(
            flops=LOCAL_FLOPS_HINT, transcendentals=1 << 20, bytes_accessed=1 << 22
        ),
        name="attend_local",
    )(bounds, queries, queries, pairs, pairs, query_seg[None, :], query_seg[:, None])


def attend_halo(queries, halo, quarters, query_seg, margin_seg, bounds, local, placement):
    row_count, width = queries.shape
    quarter = width // 4
    head_count = width // (2 * HEAD)
    slot_count = placement.shape[0]
    return pl.pallas_call(
        halo_kernel,
        out_shape=jax.ShapeDtypeStruct((slot_count, 2 * quarter), jnp.bfloat16),
        grid_spec=pltpu.PrefetchScalarGridSpec(
            num_scalar_prefetch=1,
            grid=(row_count // QUERY_BLOCK,),
            in_specs=[query_rows(quarter, q) for q in quarters]
            + [whole(2, SEG_MAX, 2 * quarter)] * 2
            + [
                query_lanes(1),
                whole(SEG_MAX, 1),
                whole(SEG_MAX, 1),
                query_lanes(2 * quarter),
                query_lanes(2, head_count),
                whole(slot_count, row_count),
            ],
            out_specs=whole(slot_count, 2 * quarter),
            scratch_shapes=[pltpu.VMEM((row_count, 2 * quarter), jnp.bfloat16)],
        ),
        compiler_params=pltpu.CompilerParams(vmem_limit_bytes=48 << 20),
        cost_estimate=pl.CostEstimate(
            flops=HALO_FLOPS_HINT, transcendentals=1 << 20, bytes_accessed=1 << 22
        ),
        name="attend_halo",
    )(
        bounds, queries, queries, *halo, query_seg[None, :], margin_seg[:SEG_MAX, None],
        margin_seg[SEG_MAX + row_count :, None], *local, placement,
    )


def key_ranges(segment_ids, query_seg, first_row):
    row_count = query_seg.shape[0]
    firsts = query_seg[::QUERY_BLOCK]
    lasts = query_seg[QUERY_BLOCK - 1 :: QUERY_BLOCK]
    low = jnp.sum((segment_ids[None, :] < firsts[:, None]).astype(jnp.int32), axis=1)
    high = jnp.sum((segment_ids[None, :] <= lasts[:, None]).astype(jnp.int32), axis=1)
    columns = []
    for start, length in ((-SEG_MAX, SEG_MAX), (0, row_count), (row_count, SEG_MAX)):
        part_low = jnp.clip(low - first_row - start, 0, length)
        part_high = jnp.clip(high - first_row - start, 0, length)
        columns += [part_low // KEY_BLOCK, (part_high + KEY_BLOCK - 1) // KEY_BLOCK]
    return jnp.stack(columns, axis=1)


def body(
    queries, keys_values, segment_ids, route_shard, route_slot, control_proj, base_hidden, cotangent
):
    row_count = queries.shape[0]
    width = queries.shape[1]
    model_width = control_proj.shape[1]
    shard_count = lax.axis_size("seq")
    shard_index = lax.axis_index("seq")
    capacity = 2 * row_count // shard_count
    slot_count = shard_count * capacity
    block_rows = width // shard_count
    far_count = shard_count // 4
    core = shard_index % 2
    near = (shard_index // 2) % 2
    far = shard_index // 4
    quarter = width // 4
    far_quarter = far_count // 4

    def swap(value, bit):
        return lax.ppermute(value, "seq", [(i, i ^ bit) for i in range(shard_count)])

    def outer(value):
        return jnp.concatenate([value[..., :quarter], value[..., 3 * quarter :]], axis=-1)

    def inner(value):
        return value[..., quarter : 3 * quarter]

    up = [(i, i + 1) for i in range(shard_count - 1)]
    down = [(j, i) for i, j in up]

    def halo(pairs):
        before = lax.ppermute(pairs[:, row_count - SEG_MAX :], "seq", up)
        after = lax.ppermute(pairs[:, :SEG_MAX], "seq", down)
        return before, after

    first_halo = halo(outer(keys_values))
    gated, first_halo = lax.optimization_barrier((inner(keys_values), first_halo))
    second_halo = halo(gated)
    peer_cotangent = swap(cotangent, 1)

    target_shard = route_shard[:, 0]
    one_hot = (target_shard[:, None] == jnp.arange(shard_count, dtype=jnp.int32)[None, :]).astype(
        jnp.int32
    )
    slot_rank = jnp.sum((jnp.cumsum(one_hot, axis=0) - 1) * one_hot, axis=1)
    flat_place = target_shard * capacity + slot_rank
    place_mask = flat_place[None, :] == jnp.arange(slot_count, dtype=jnp.int32)[:, None]
    placement = place_mask.astype(jnp.bfloat16)
    occupied = jnp.sum(place_mask.astype(jnp.int32), axis=1)
    slot_values = jnp.sum(jnp.where(place_mask, route_slot[None, :], 0), axis=1)
    slot_table = jnp.where(occupied > 0, slot_values, -1).reshape(shard_count, capacity)
    incoming_slots = lax.all_to_all(slot_table, "seq", split_axis=0, concat_axis=0, tiled=True)
    landing = (
        incoming_slots.reshape(-1)[:, None] == jnp.arange(row_count, dtype=jnp.int32)[None, :]
    ).astype(jnp.bfloat16)

    first_row = shard_index * row_count
    query_seg = lax.dynamic_slice_in_dim(segment_ids, first_row, row_count)
    padded_seg = jnp.pad(segment_ids, (SEG_MAX, SEG_MAX), constant_values=-1)
    key_seg = lax.dynamic_slice_in_dim(padded_seg, first_row, row_count + 2 * SEG_MAX)
    bounds = key_ranges(segment_ids, query_seg, first_row)
    quarters = ((0, 3), (1, 2))
    outer_local = attend_local(queries, keys_values, quarters[0], query_seg, bounds)
    inner_local = attend_local(queries, keys_values, quarters[1], query_seg, bounds)
    outer_local, inner_local, first_halo = lax.optimization_barrier(
        (outer_local, inner_local, first_halo)
    )
    outer_placed = attend_halo(
        queries, first_halo, quarters[0], query_seg, key_seg, bounds, outer_local, placement
    )
    inner_placed = attend_halo(
        queries, second_halo, quarters[1], query_seg, key_seg, bounds, inner_local, placement
    )

    def split_columns(parts):
        step = model_width // parts
        return [slice(part * step, (part + 1) * step) for part in range(parts)]

    def product(halves, columns):
        return sum(
            jnp.einsum("fbt,td->fbd", half, other[:, columns], preferred_element_type=jnp.float32)
            for half, other in zip(halves, (cotangent, peer_cotangent))
        )

    def land(value):
        incoming = lax.all_to_all(
            value.reshape(shard_count, capacity, 2 * quarter),
            "seq",
            split_axis=0,
            concat_axis=0,
            tiled=True,
        )
        return jnp.einsum(
            "sk,sr->kr",
            incoming.reshape(slot_count, 2 * quarter),
            landing,
            preferred_element_type=jnp.float32,
        ).astype(jnp.bfloat16)

    def near_reduce(rows, parts):
        by_core = rows.reshape(far_count, 2, block_rows, row_count)
        peer_rows = swap(lax.dynamic_index_in_dim(by_core, 1 - core, 1, keepdims=False), 1)
        own_rows = lax.dynamic_index_in_dim(by_core, core, 1, keepdims=False)
        by_near = [
            value.reshape(far_count // 2, 2, block_rows, row_count) for value in (own_rows, peer_rows)
        ]
        sent_rows = [lax.dynamic_index_in_dim(v, 1 - near, 1, keepdims=False) for v in by_near]
        kept_rows = [lax.dynamic_index_in_dim(v, near, 1, keepdims=False) for v in by_near]
        sent = [product(sent_rows, columns).astype(jnp.bfloat16) for columns in split_columns(parts)]
        summed = [
            product(kept_rows, columns) + swap(value, 2).astype(jnp.float32)
            for columns, value in zip(split_columns(parts), sent)
        ]
        return sent, summed

    def far_exchange(chunk, summed):
        members = [
            f for f in range(far_count) if (far_quarter <= f < 3 * far_quarter) == (chunk == 1)
        ]

        def place_of(index):
            if chunk == 1:
                return index - far_quarter
            return jnp.where(index < far_quarter, index, index - 2 * far_quarter)

        kept = lax.dynamic_index_in_dim(summed, place_of(far), 0, keepdims=False)
        rounded = summed.astype(jnp.bfloat16)
        arrived = []
        for other in range(1, far_count):
            piece = lax.dynamic_index_in_dim(rounded, place_of(far ^ other), 0, keepdims=False)
            routes = [
                (i, i ^ (4 * other)) for i in range(shard_count) if (i // 4) ^ other in members
            ]
            arrived.append(lax.ppermute(piece, "seq", routes))
        return kept, arrived

    def far_total(kept, arrived):
        return kept + sum(value.astype(jnp.float32) for value in arrived)

    outer_rows = land(outer_placed)
    _, outer_summed = near_reduce(outer_rows, OUTER_PARTS)
    outer_far = [far_exchange(0, value) for value in outer_summed]
    inner_rows = land(inner_placed)
    _, inner_summed = near_reduce(inner_rows, INNER_PARTS)
    outer_far, late_rows, inner_summed[0] = lax.optimization_barrier(
        (outer_far, inner_rows, inner_summed[0])
    )
    inner_far = [far_exchange(1, value) for value in inner_summed]
    grad_parts = [
        jnp.concatenate([far_total(*pair) for pair in pairs], axis=1)
        for pairs in (outer_far, inner_far)
    ]
    in_middle = (far >= far_quarter) & (far < 3 * far_quarter)
    proj_grad = jnp.where(in_middle, grad_parts[1], grad_parts[0])

    added = jnp.einsum(
        "kr,kd->rd",
        jnp.concatenate([outer_rows[:quarter], late_rows, outer_rows[quarter:]], axis=0),
        control_proj,
        preferred_element_type=jnp.float32,
    )
    mixed_hidden = (base_hidden.astype(jnp.float32) + added).astype(jnp.bfloat16)
    return (mixed_hidden, proj_grad)


def solution(mesh):
    placed = (
        P(("grp", "seq"), None),
        P(None, ("grp", "seq"), None),
        P("grp"),
        P(("grp", "seq"), None),
        P(("grp", "seq")),
        P(),
        P(("grp", "seq"), None),
        P(("grp", "seq"), None),
    )
    return jax.shard_map(
        body,
        mesh=mesh,
        in_specs=placed,
        out_specs=(P(("grp", "seq"), None), P(("grp", "seq"), None)),
        check_vma=False,
    )
```

profile of v0, /device:TPU:10, one launch (start us, length us, event | category | flops | bytes accessed | tf_op | source)
XLA Modules:
  0.0 227.3 jit_solution(6231912036174468854)
XLA Ops:
  3.5 2.0 collective-permute-start
  5.5 4.5 %collective-permute-start.1 = (bf16[2,512,768]{2,1,0:T(8,128)(2,1)}, bf16[2,512,768]{2,1,0:T(8,128)(2,1)}, u32[]{:S(2)}, u32[]{:S(2)}) collective-permute-start(bf16[2,512,768]{2,1,0:T(8,128)(2,1)} %pad_maximum_fusion), channel_id=1, source_target_pairs={{1,0},{2,1},{3,2},{4,3},{5,4},{6,5},{7,6},{8,7},{9,8},{10,9},{11,1... | collective-permute-start | bytes 4718600 | tf_op jit(solution)/shard_map/ppermute | solution.py:245
  13.0 5.4 %all-to-all-start.1 = ((s32[16,1,64]{2,1,0:T(1,128)}), s32[16,1,64]{2,1,0:T(1,128)S(1)}, u32[]{:S(2)}, u32[]{:S(2)}) async-start(s32[16,1,64]{2,1,0:T(1,128)} %select_n.195), calls=%async_computation.1 | async-start | bytes 16384 | tf_op jit(solution)/shard_map/all_to_all | solution.py:264
  21.8 7.5 %attend_local.3 = (f32[768,512]{1,0:T(8,128)S(1)}, f32[2,6,512]{2,1,0:T(8,128)S(1)}) custom-call(s32[4,6]{1,0:T(4,128)S(1)} %stack.2.bounds, bf16[512,1536]{1,0:T(8,128)(2,1)S(1)} %copy-done, bf16[512,1536]{1,0:T(8,128)(2,1)S(1)} %copy-done, bf16[2,512,1536]{2,1,0:T(8,128)(2,1)} %last_own_ref.3, bf16[2,512,1536]{2,1,0:T(8,128)(2,1)} %last_own_ref.3, ...), custom_call_target="tpu_custom_call" | custom-call | flops 8589934592 | bytes 4194304 | tf_op jit(solution)/shard_map/attend_local/pallas_call | solution.py:142
  29.4 7.5 %attend_local.2 = (f32[768,512]{1,0:T(8,128)S(1)}, f32[2,6,512]{2,1,0:T(8,128)S(1)}) custom-call(s32[4,6]{1,0:T(4,128)S(1)} %stack.2.bounds, bf16[512,1536]{1,0:T(8,128)(2,1)S(1)} %copy-done, bf16[512,1536]{1,0:T(8,128)(2,1)S(1)} %copy-done, bf16[2,512,1536]{2,1,0:T(8,128)(2,1)} %last_own_ref.3, bf16[2,512,1536]{2,1,0:T(8,128)(2,1)} %last_own_ref.3, ...), custom_call_target="tpu_custom_call" | custom-call | flops 8589934592 | bytes 4194304 | tf_op jit(solution)/shard_map/attend_local/pallas_call | solution.py:142
  38.1 7.1 %collective-permute-start.12 = (bf16[2,512,768]{2,1,0:T(8,128)(2,1)}, bf16[2,512,768]{2,1,0:T(8,128)(2,1)}, u32[]{:S(2)}, u32[]{:S(2)}) collective-permute-start(bf16[2,512,768]{2,1,0:T(8,128)(2,1)} %slice.61), channel_id=1, source_target_pairs={{0,1},{1,2},{2,3},{3,4},{4,5},{5,6},{6,7},{7,8},{8,9},{9,10},{10,1... | collective-permute-start | bytes 4718600 | tf_op jit(solution)/shard_map/ppermute | solution.py:244
  47.1 8.3 %attend_halo.2 = bf16[1024,768]{1,0:T(8,128)(2,1)} custom-call(s32[4,6]{1,0:T(4,128)S(1)} %stack.2.bounds, bf16[512,1536]{1,0:T(8,128)(2,1)S(1)} %copy-done, bf16[512,1536]{1,0:T(8,128)(2,1)S(1)} %copy-done, bf16[2,512,768]{2,1,0:T(8,128)(2,1)} %collective-permute-done.before_ref, bf16[2,512,768]{2,1,0:T(8,128)(2,1)} %collective-permute-done.1.after_ref, ...), custom_call_target="tpu_custom_call" | custom-call | flops 17179869184 | bytes 4194304 | tf_op jit(solution)/shard_map/attend_halo/pallas_call | solution.py:169
  55.5 8.7 %all-to-all-start = ((bf16[16,64,768]{2,1,0:T(8,128)(2,1)}), bf16[16,64,768]{2,1,0:T(8,128)(2,1)}, u32[]{:S(2)}, u32[]{:S(2)}) async-start(bf16[16,64,768]{2,1,0:T(8,128)(2,1)} %bitcast.13), calls=%async_computation | async-start | bytes 3145728 | tf_op jit(solution)/shard_map/all_to_all | solution.py:298
  65.8 8.3 %attend_halo.3 = bf16[1024,768]{1,0:T(8,128)(2,1)} custom-call(s32[4,6]{1,0:T(4,128)S(1)} %stack.2.bounds, bf16[512,1536]{1,0:T(8,128)(2,1)S(1)} %copy-done, bf16[512,1536]{1,0:T(8,128)(2,1)S(1)} %copy-done, bf16[2,512,768]{2,1,0:T(8,128)(2,1)} %collective-permute-done.12.before_ref, bf16[2,512,768]{2,1,0:T(8,128)(2,1)} %collective-permute-done.13.after_ref, ...), custom_call_target="tpu_custom_call" | custom-call | flops 17179869184 | bytes 4194304 | tf_op jit(solution)/shard_map/attend_halo/pallas_call | solution.py:169
  74.1 25.1 %all-to-all-done = bf16[16,64,768]{2,1,0:T(8,128)(2,1)} async-done(((bf16[16,64,768]{2,1,0:T(8,128)(2,1)}), bf16[16,64,768]{2,1,0:T(8,128)(2,1)}, u32[]{:S(2)}, u32[]{:S(2)}) %all-to-all-start) | async-done | bytes 1572896 | tf_op jit(solution)/shard_map/all_to_all | solution.py:298
  99.2 11.4 %all-to-all-start.2 = ((bf16[16,64,768]{2,1,0:T(8,128)(2,1)}), bf16[16,64,768]{2,1,0:T(8,128)(2,1)}, u32[]{:S(2)}, u32[]{:S(2)}) async-start(bf16[16,64,768]{2,1,0:T(8,128)(2,1)} %bitcast.35), calls=%async_computation.2 | async-start | bytes 3145728 | tf_op jit(solution)/shard_map/all_to_all | solution.py:298
  110.6 2.7 %fusion.32 = bf16[768,512]{1,0:T(8,128)(2,1)S(1)} fusion(bf16[1024,768]{1,0:T(8,128)(2,1)} %bitcast.14, s32[1024]{0:T(1024)S(1)} %eq.64), kind=kOutput, calls=%fused_computation.48 | convolution fusion | flops 806223872 | bytes 2363392 | tf_op jit(solution)/shard_map/sk,sr->kr/dot_general | solution.py:305
  122.4 20.1 %collective-permute-done.8 = bf16[2,96,1536]{2,1,0:T(8,128)(2,1)S(1)} collective-permute-done((bf16[2,96,1536]{2,1,0:T(8,128)(2,1)S(1)}, bf16[2,96,1536]{2,1,0:T(8,128)(2,1)S(1)}, u32[]{:S(2)}, u32[]{:S(2)}) %collective-permute-start.8) | collective-permute-done | bytes 589856 | tf_op jit(solution)/shard_map/ppermute | solution.py:232
  145.4 5.0 %collective-permute-start.10 = (bf16[96,1536]{1,0:T(8,128)(2,1)}, bf16[96,1536]{1,0:T(8,128)(2,1)}, u32[]{:S(2)}, u32[]{:S(2)}) collective-permute-start(bf16[96,1536]{1,0:T(8,128)(2,1)} %get-tuple-element.67), channel_id=1, source_target_pairs={{4,12},{5,13},{6,14},{7,15},{8,0},{9,1},{10,2},{11,3},{20,28},{21,... | collective-permute-start | bytes 884744 | tf_op jit(solution)/shard_map/ppermute | solution.py:346
  151.8 3.3 %collective-permute-start.9 = (bf16[96,1536]{1,0:T(8,128)(2,1)}, bf16[96,1536]{1,0:T(8,128)(2,1)}, u32[]{:S(2)}, u32[]{:S(2)}) collective-permute-start(bf16[96,1536]{1,0:T(8,128)(2,1)} %get-tuple-element.68), channel_id=1, source_target_pairs={{4,0},{5,1},{6,2},{7,3},{8,12},{9,13},{10,14},{11,15},{20,16},{21,... | collective-permute-start | bytes 884744 | tf_op jit(solution)/shard_map/ppermute | solution.py:346
  163.2 2.5 %fusion.33 = bf16[768,512]{1,0:T(8,128)(2,1)S(1)} fusion(bf16[1024,768]{1,0:T(8,128)(2,1)} %bitcast.36, s32[1024]{0:T(1024)S(1)} %eq.64), kind=kOutput, calls=%fused_computation.49 | convolution fusion | flops 806223872 | bytes 2363392 | tf_op jit(solution)/shard_map/sk,sr->kr/dot_general | solution.py:305
  170.2 2.3 %collective-permute-start.15 = (bf16[2,96,1536]{2,1,0:T(8,128)(2,1)S(1)}, bf16[2,96,1536]{2,1,0:T(8,128)(2,1)S(1)}, u32[]{:S(2)}, u32[]{:S(2)}) collective-permute-start(bf16[2,96,1536]{2,1,0:T(8,128)(2,1)S(1)} %fusion.6), channel_id=1, source_target_pairs={{0,2},{1,3},{2,0},{3,1},{4,6},{5,7},{6,4},{7,5},{8,10},{9,11},{10,... | collective-permute-start | bytes 1769480 | tf_op jit(solution)/shard_map/ppermute | solution.py:232
  177.0 9.1 %collective-permute-done.15 = bf16[2,96,1536]{2,1,0:T(8,128)(2,1)S(1)} collective-permute-done((bf16[2,96,1536]{2,1,0:T(8,128)(2,1)S(1)}, bf16[2,96,1536]{2,1,0:T(8,128)(2,1)S(1)}, u32[]{:S(2)}, u32[]{:S(2)}) %collective-permute-start.15) | collective-permute-done | bytes 589856 | tf_op jit(solution)/shard_map/ppermute | solution.py:232
  192.7 2.9 %collective-permute-start.18 = (bf16[96,1536]{1,0:T(8,128)(2,1)S(1)}, bf16[96,1536]{1,0:T(8,128)(2,1)S(1)}, u32[]{:S(2)}, u32[]{:S(2)}) collective-permute-start(bf16[96,1536]{1,0:T(8,128)(2,1)S(1)} %get-tuple-element.61), channel_id=1, source_target_pairs={{4,8},{5,9},{6,10},{7,11},{8,4},{9,5},{10,6},{11,7},{20,24},{21,25... | collective-permute-start | bytes 884744 | tf_op jit(solution)/shard_map/ppermute | solution.py:346
  195.6 5.4 %collective-permute-done.19 = bf16[2,96,1536]{2,1,0:T(8,128)(2,1)S(1)} collective-permute-done((bf16[2,96,1536]{2,1,0:T(8,128)(2,1)S(1)}, bf16[2,96,1536]{2,1,0:T(8,128)(2,1)S(1)}, u32[]{:S(2)}, u32[]{:S(2)}) %collective-permute-start.19) | collective-permute-done | bytes 589856 | tf_op jit(solution)/shard_map/ppermute | solution.py:232
  201.0 2.1 fusion.112
  207.3 6.7 %add_convert_fusion = bf16[512,3072]{1,0:T(8,128)(2,1)} fusion(bf16[512,3072]{1,0:T(8,128)(2,1)S(1)} %copy-done.13, bf16[1536,3072]{1,0:T(8,128)(2,1)S(1)} %bitcast.197, bf16[384,512]{1,0:T(8,128)(2,1)S(1)} %copy-done.7, bf16[768,512]{1,0:T(8,128)(2,1)S(1)} %fusion.33, bf16[384,512]{1,0:T(8,128)(2,1)S(1)} %get-tuple-element.54), kind=kOutput, calls=%fused_computation | convolution fusion | flops 4841275392 | bytes 17301504 | tf_op jit(solution)/shard_map/kr,kd->rd/dot_general | solution.py:368
  215.3 3.4 %collective-permute-start.22 = (bf16[96,1536]{1,0:T(8,128)(2,1)S(1)}, bf16[96,1536]{1,0:T(8,128)(2,1)S(1)}, u32[]{:S(2)}, u32[]{:S(2)}) collective-permute-start(bf16[96,1536]{1,0:T(8,128)(2,1)S(1)} %get-tuple-element.64), channel_id=1, source_target_pairs={{4,8},{5,9},{6,10},{7,11},{8,4},{9,5},{10,6},{11,7},{20,24},{21,25... | collective-permute-start | bytes 884744 | tf_op jit(solution)/shard_map/ppermute | solution.py:346
  219.8 6.2 %collective-permute-done.22 = bf16[96,1536]{1,0:T(8,128)(2,1)S(1)} collective-permute-done((bf16[96,1536]{1,0:T(8,128)(2,1)S(1)}, bf16[96,1536]{1,0:T(8,128)(2,1)S(1)}, u32[]{:S(2)}, u32[]{:S(2)}) %collective-permute-start.22) | collective-permute-done | bytes 294944 | tf_op jit(solution)/shard_map/ppermute | solution.py:346
  (137 shorter events, 58.3 us)
Async XLA Ops:
  3.5 34.6 %collective-permute-start = (bf16[2,512,768]{2,1,0:T(8,128)(2,1)}, bf16[2,512,768]{2,1,0:T(8,128)(2,1)}, u32[]{:S(2)}, u32[]{:S(2)}) collective-permute-start(bf16[2,512,768]{2,1,0:T(8,128)(2,1)} %pad_maximum_fusion), channel_id=1, source_target_pairs={{0,1},{1,2},{2,3},{3,4},{4,5},{5,6},{6,7},{7,8},{8,9},{9,10},{10,1... | collective-permute-start | bytes 4718600 | tf_op jit(solution)/shard_map/ppermute | solution.py:244
  5.5 32.5 %collective-permute-start.1 = (bf16[2,512,768]{2,1,0:T(8,128)(2,1)}, bf16[2,512,768]{2,1,0:T(8,128)(2,1)}, u32[]{:S(2)}, u32[]{:S(2)}) collective-permute-start(bf16[2,512,768]{2,1,0:T(8,128)(2,1)} %pad_maximum_fusion), channel_id=1, source_target_pairs={{1,0},{2,1},{3,2},{4,3},{5,4},{6,5},{7,6},{8,7},{9,8},{10,9},{11,1... | collective-permute-start | bytes 4718600 | tf_op jit(solution)/shard_map/ppermute | solution.py:245
  13.0 42.5 %all-to-all-start.1 = ((s32[16,1,64]{2,1,0:T(1,128)}), s32[16,1,64]{2,1,0:T(1,128)S(1)}, u32[]{:S(2)}, u32[]{:S(2)}) async-start(s32[16,1,64]{2,1,0:T(1,128)} %select_n.195), calls=%async_computation.1 | async-start | bytes 16384 | tf_op jit(solution)/shard_map/all_to_all | solution.py:264
  38.1 27.5 %collective-permute-start.12 = (bf16[2,512,768]{2,1,0:T(8,128)(2,1)}, bf16[2,512,768]{2,1,0:T(8,128)(2,1)}, u32[]{:S(2)}, u32[]{:S(2)}) collective-permute-start(bf16[2,512,768]{2,1,0:T(8,128)(2,1)} %slice.61), channel_id=1, source_target_pairs={{0,1},{1,2},{2,3},{3,4},{4,5},{5,6},{6,7},{7,8},{8,9},{9,10},{10,1... | collective-permute-start | bytes 4718600 | tf_op jit(solution)/shard_map/ppermute | solution.py:244
  45.2 20.5 %collective-permute-start.13 = (bf16[2,512,768]{2,1,0:T(8,128)(2,1)}, bf16[2,512,768]{2,1,0:T(8,128)(2,1)}, u32[]{:S(2)}, u32[]{:S(2)}) collective-permute-start(bf16[2,512,768]{2,1,0:T(8,128)(2,1)} %slice.61), channel_id=1, source_target_pairs={{1,0},{2,1},{3,2},{4,3},{5,4},{6,5},{7,6},{8,7},{9,8},{10,9},{11,1... | collective-permute-start | bytes 4718600 | tf_op jit(solution)/shard_map/ppermute | solution.py:245
  55.5 43.7 %all-to-all-start = ((bf16[16,64,768]{2,1,0:T(8,128)(2,1)}), bf16[16,64,768]{2,1,0:T(8,128)(2,1)}, u32[]{:S(2)}, u32[]{:S(2)}) async-start(bf16[16,64,768]{2,1,0:T(8,128)(2,1)} %bitcast.13), calls=%async_computation | async-start | bytes 3145728 | tf_op jit(solution)/shard_map/all_to_all | solution.py:298
  64.2 51.8 %collective-permute-start.3 = (bf16[512,3072]{1,0:T(8,128)(2,1)}, bf16[512,3072]{1,0:T(8,128)(2,1)}, u32[]{:S(2)}, u32[]{:S(2)}) collective-permute-start(bf16[512,3072]{1,0:T(8,128)(2,1)} %param.15), channel_id=1, source_target_pairs={{0,1},{1,0},{2,3},{3,2},{4,5},{5,4},{6,7},{7,6},{8,9},{9,8},{10,11... | collective-permute-start | bytes 9437192 | tf_op jit(solution)/shard_map/ppermute | solution.py:232
  99.2 64.1 %all-to-all-start.2 = ((bf16[16,64,768]{2,1,0:T(8,128)(2,1)}), bf16[16,64,768]{2,1,0:T(8,128)(2,1)}, u32[]{:S(2)}, u32[]{:S(2)}) async-start(bf16[16,64,768]{2,1,0:T(8,128)(2,1)} %bitcast.35), calls=%async_computation.2 | async-start | bytes 3145728 | tf_op jit(solution)/shard_map/all_to_all | solution.py:298
  117.9 24.7 %collective-permute-start.8 = (bf16[2,96,1536]{2,1,0:T(8,128)(2,1)S(1)}, bf16[2,96,1536]{2,1,0:T(8,128)(2,1)S(1)}, u32[]{:S(2)}, u32[]{:S(2)}) collective-permute-start(bf16[2,96,1536]{2,1,0:T(8,128)(2,1)S(1)} %fusion.5), channel_id=1, source_target_pairs={{0,2},{1,3},{2,0},{3,1},{4,6},{5,7},{6,4},{7,5},{8,10},{9,11},{10,... | collective-permute-start | bytes 1769480 | tf_op jit(solution)/shard_map/ppermute | solution.py:232
  121.8 34.9 %collective-permute-start.4 = (bf16[2,96,1536]{2,1,0:T(8,128)(2,1)S(1)}, bf16[2,96,1536]{2,1,0:T(8,128)(2,1)S(1)}, u32[]{:S(2)}, u32[]{:S(2)}) collective-permute-start(bf16[2,96,1536]{2,1,0:T(8,128)(2,1)S(1)} %fusion.4), channel_id=1, source_target_pairs={{0,2},{1,3},{2,0},{3,1},{4,6},{5,7},{6,4},{7,5},{8,10},{9,11},{10,... | collective-permute-start | bytes 1769480 | tf_op jit(solution)/shard_map/ppermute | solution.py:232
  145.4 29.6 %collective-permute-start.10 = (bf16[96,1536]{1,0:T(8,128)(2,1)}, bf16[96,1536]{1,0:T(8,128)(2,1)}, u32[]{:S(2)}, u32[]{:S(2)}) collective-permute-start(bf16[96,1536]{1,0:T(8,128)(2,1)} %get-tuple-element.67), channel_id=1, source_target_pairs={{4,12},{5,13},{6,14},{7,15},{8,0},{9,1},{10,2},{11,3},{20,28},{21,... | collective-permute-start | bytes 884744 | tf_op jit(solution)/shard_map/ppermute | solution.py:346
  150.4 25.9 %collective-permute-start.11 = (bf16[96,1536]{1,0:T(8,128)(2,1)}, bf16[96,1536]{1,0:T(8,128)(2,1)}, u32[]{:S(2)}, u32[]{:S(2)}) collective-permute-start(bf16[96,1536]{1,0:T(8,128)(2,1)} %get-tuple-element.66), channel_id=1, source_target_pairs={{0,12},{1,13},{2,14},{3,15},{12,0},{13,1},{14,2},{15,3},{16,28},{1... | collective-permute-start | bytes 884744 | tf_op jit(solution)/shard_map/ppermute | solution.py:346
  151.8 38.0 %collective-permute-start.9 = (bf16[96,1536]{1,0:T(8,128)(2,1)}, bf16[96,1536]{1,0:T(8,128)(2,1)}, u32[]{:S(2)}, u32[]{:S(2)}) collective-permute-start(bf16[96,1536]{1,0:T(8,128)(2,1)} %get-tuple-element.68), channel_id=1, source_target_pairs={{4,0},{5,1},{6,2},{7,3},{8,12},{9,13},{10,14},{11,15},{20,16},{21,... | collective-permute-start | bytes 884744 | tf_op jit(solution)/shard_map/ppermute | solution.py:346
  159.5 30.3 %collective-permute-start.5 = (bf16[96,1536]{1,0:T(8,128)(2,1)}, bf16[96,1536]{1,0:T(8,128)(2,1)}, u32[]{:S(2)}, u32[]{:S(2)}) collective-permute-start(bf16[96,1536]{1,0:T(8,128)(2,1)} %get-tuple-element.71), channel_id=1, source_target_pairs={{4,0},{5,1},{6,2},{7,3},{8,12},{9,13},{10,14},{11,15},{20,16},{21,... | collective-permute-start | bytes 884744 | tf_op jit(solution)/shard_map/ppermute | solution.py:346
  170.2 15.9 %collective-permute-start.15 = (bf16[2,96,1536]{2,1,0:T(8,128)(2,1)S(1)}, bf16[2,96,1536]{2,1,0:T(8,128)(2,1)S(1)}, u32[]{:S(2)}, u32[]{:S(2)}) collective-permute-start(bf16[2,96,1536]{2,1,0:T(8,128)(2,1)S(1)} %fusion.6), channel_id=1, source_target_pairs={{0,2},{1,3},{2,0},{3,1},{4,6},{5,7},{6,4},{7,5},{8,10},{9,11},{10,... | collective-permute-start | bytes 1769480 | tf_op jit(solution)/shard_map/ppermute | solution.py:232
  175.0 14.8 %collective-permute-start.6 = (bf16[96,1536]{1,0:T(8,128)(2,1)S(1)}, bf16[96,1536]{1,0:T(8,128)(2,1)S(1)}, u32[]{:S(2)}, u32[]{:S(2)}) collective-permute-start(bf16[96,1536]{1,0:T(8,128)(2,1)S(1)} %copy-done.9), channel_id=1, source_target_pairs={{4,12},{5,13},{6,14},{7,15},{8,0},{9,1},{10,2},{11,3},{20,28},{21,... | collective-permute-start | bytes 884744 | tf_op jit(solution)/shard_map/ppermute | solution.py:346
  176.3 13.5 %collective-permute-start.7 = (bf16[96,1536]{1,0:T(8,128)(2,1)S(1)}, bf16[96,1536]{1,0:T(8,128)(2,1)S(1)}, u32[]{:S(2)}, u32[]{:S(2)}) collective-permute-start(bf16[96,1536]{1,0:T(8,128)(2,1)S(1)} %copy-done.8), channel_id=1, source_target_pairs={{0,12},{1,13},{2,14},{3,15},{12,0},{13,1},{14,2},{15,3},{16,28},{1... | collective-permute-start | bytes 884744 | tf_op jit(solution)/shard_map/ppermute | solution.py:346
  186.1 14.9 %collective-permute-start.19 = (bf16[2,96,1536]{2,1,0:T(8,128)(2,1)S(1)}, bf16[2,96,1536]{2,1,0:T(8,128)(2,1)S(1)}, u32[]{:S(2)}, u32[]{:S(2)}) collective-permute-start(bf16[2,96,1536]{2,1,0:T(8,128)(2,1)S(1)} %fusion.7), channel_id=1, source_target_pairs={{0,2},{1,3},{2,0},{3,1},{4,6},{5,7},{6,4},{7,5},{8,10},{9,11},{10,... | collective-permute-start | bytes 1769480 | tf_op jit(solution)/shard_map/ppermute | solution.py:232
  190.0 25.3 %collective-permute-start.16 = (bf16[96,1536]{1,0:T(8,128)(2,1)S(1)}, bf16[96,1536]{1,0:T(8,128)(2,1)S(1)}, u32[]{:S(2)}, u32[]{:S(2)}) collective-permute-start(bf16[96,1536]{1,0:T(8,128)(2,1)S(1)} %get-tuple-element.60), channel_id=1, source_target_pairs={{0,4},{1,5},{2,6},{3,7},{12,8},{13,9},{14,10},{15,11},{16,20},{17,... | collective-permute-start | bytes 884744 | tf_op jit(solution)/shard_map/ppermute | solution.py:346
  191.4 27.2 %collective-permute-start.17 = (bf16[96,1536]{1,0:T(8,128)(2,1)S(1)}, bf16[96,1536]{1,0:T(8,128)(2,1)S(1)}, u32[]{:S(2)}, u32[]{:S(2)}) collective-permute-start(bf16[96,1536]{1,0:T(8,128)(2,1)S(1)} %get-tuple-element.62), channel_id=1, source_target_pairs={{0,8},{1,9},{2,10},{3,11},{12,4},{13,5},{14,6},{15,7},{16,24},{17,... | collective-permute-start | bytes 884744 | tf_op jit(solution)/shard_map/ppermute | solution.py:346
  192.7 25.9 %collective-permute-start.18 = (bf16[96,1536]{1,0:T(8,128)(2,1)S(1)}, bf16[96,1536]{1,0:T(8,128)(2,1)S(1)}, u32[]{:S(2)}, u32[]{:S(2)}) collective-permute-start(bf16[96,1536]{1,0:T(8,128)(2,1)S(1)} %get-tuple-element.61), channel_id=1, source_target_pairs={{4,8},{5,9},{6,10},{7,11},{8,4},{9,5},{10,6},{11,7},{20,24},{21,25... | collective-permute-start | bytes 884744 | tf_op jit(solution)/shard_map/ppermute | solution.py:346
  203.2 15.7 %collective-permute-start.20 = (bf16[96,1536]{1,0:T(8,128)(2,1)S(1)}, bf16[96,1536]{1,0:T(8,128)(2,1)S(1)}, u32[]{:S(2)}, u32[]{:S(2)}) collective-permute-start(bf16[96,1536]{1,0:T(8,128)(2,1)S(1)} %get-tuple-element.63), channel_id=1, source_target_pairs={{0,4},{1,5},{2,6},{3,7},{12,8},{13,9},{14,10},{15,11},{16,20},{17,... | collective-permute-start | bytes 884744 | tf_op jit(solution)/shard_map/ppermute | solution.py:346
  204.6 15.2 %collective-permute-start.21 = (bf16[96,1536]{1,0:T(8,128)(2,1)S(1)}, bf16[96,1536]{1,0:T(8,128)(2,1)S(1)}, u32[]{:S(2)}, u32[]{:S(2)}) collective-permute-start(bf16[96,1536]{1,0:T(8,128)(2,1)S(1)} %get-tuple-element.65), channel_id=1, source_target_pairs={{0,8},{1,9},{2,10},{3,11},{12,4},{13,5},{14,6},{15,7},{16,24},{17,... | collective-permute-start | bytes 884744 | tf_op jit(solution)/shard_map/ppermute | solution.py:346
  215.3 10.7 %collective-permute-start.22 = (bf16[96,1536]{1,0:T(8,128)(2,1)S(1)}, bf16[96,1536]{1,0:T(8,128)(2,1)S(1)}, u32[]{:S(2)}, u32[]{:S(2)}) collective-permute-start(bf16[96,1536]{1,0:T(8,128)(2,1)S(1)} %get-tuple-element.64), channel_id=1, source_target_pairs={{4,8},{5,9},{6,10},{7,11},{8,4},{9,5},{10,6},{11,7},{20,24},{21,25... | collective-permute-start | bytes 884744 | tf_op jit(solution)/shard_map/ppermute | solution.py:346
  (19 other events, 193.0 us)
where the time goes:
time: 229 us; the launch traced here: 227 us
  starting transfers between devices  73.4 us (32%)
  waiting for transfers between devices  69.3 us (30%)
  Pallas kernels  31.7 us (14%)
  matrix products  31.4 us (14%)
  local copies, waits for them, and re-layouts  11.6 us (5%)
  other arithmetic  8.46 us (4%)
    ppermute x7, waiting for transfers between devices, swap(): lax.ppermute(value, 'seq', [(i, i ^ bit) for i in range(shard_count)])  36.8 us
    ppermute x12, starting transfers between devices, far_exchange(): arrived.append(lax.ppermute(piece, 'seq', routes))  25.6 us
    all_to_all x2, waiting for transfers between devices, land(): lax.all_to_all(value.reshape(shard_count, capacity, 2 * quarter), 'seq',...  25.1 us
    all_to_all x2, starting transfers between devices, land(): lax.all_to_all(value.reshape(shard_count, capacity, 2 * quarter), 'seq',...  20.1 us
    dot_general x16, matrix products, product(): jnp.einsum('fbt,td->fbd', half, other[:, columns], preferred_element_type...  19.5 us
    pallas_call x2, Pallas kernels, attend_halo(): pl.pallas_call(halo_kernel, out_shape=jax.ShapeDtypeStruct((slot_count, 2...  16.7 us
    pallas_call x2, Pallas kernels, attend_local(): pl.pallas_call(local_kernel, out_shape=(jax.ShapeDtypeStruct((2 * quarter...  15.1 us
    ppermute x2, starting transfers between devices, halo(): before = lax.ppermute(pairs[:, row_count - SEG_MAX:], 'seq', up)  9.17 us
  transfers between devices with their start and end apart: 26, of which 9 were waited for; matrix products, arithmetic and copies ran while one was open for 20% of the time, Pallas kernels for 14%

commit v1 on v0

--- a/solution.py
+++ b/solution.py
@@ -309,23 +309,48 @@
             preferred_element_type=jnp.float32,
         ).astype(jnp.bfloat16)
 
-    def near_reduce(rows, parts):
+    def near_parts(rows):
         by_core = rows.reshape(far_count, 2, block_rows, row_count)
         peer_rows = swap(lax.dynamic_index_in_dim(by_core, 1 - core, 1, keepdims=False), 1)
         own_rows = lax.dynamic_index_in_dim(by_core, core, 1, keepdims=False)
         by_near = [
             value.reshape(far_count // 2, 2, block_rows, row_count) for value in (own_rows, peer_rows)
         ]
-        sent_rows = [lax.dynamic_index_in_dim(v, 1 - near, 1, keepdims=False) for v in by_near]
-        kept_rows = [lax.dynamic_index_in_dim(v, near, 1, keepdims=False) for v in by_near]
+        return [
+            [lax.dynamic_index_in_dim(v, which, 1, keepdims=False) for v in by_near]
+            for which in (1 - near, near)
+        ]
+
+    def near_exchange(sent_rows, parts):
         sent = [product(sent_rows, columns).astype(jnp.bfloat16) for columns in split_columns(parts)]
-        summed = [
-            product(kept_rows, columns) + swap(value, 2).astype(jnp.float32)
-            for columns, value in zip(split_columns(parts), sent)
+        return sent, [swap(value, 2) for value in sent]
+
+    def near_sum(kept_rows, arrived):
+        return [
+            product(kept_rows, columns) + value.astype(jnp.float32)
+            for columns, value in zip(split_columns(len(arrived)), arrived)
         ]
-        return sent, summed
-
-    def far_exchange(chunk, summed):
+
+    def line_exchange(chunk, summed, rounded):
+        def pick(value, holder):
+            return lax.dynamic_index_in_dim(
+                value, jnp.where(far == holder, 1, 0), 0, keepdims=False
+            )
+
+        def hop(piece, moves):
+            routes = [(4 * a + i, 4 * b + i) for a, b in moves for i in range(4)]
+            return lax.ppermute(piece, "seq", routes)
+
+        def add(holder, arrived):
+            return (pick(summed, holder) + arrived.astype(jnp.float32)).astype(jnp.bfloat16)
+
+        inward = hop(pick(rounded, 0), ((0, 1), (3, 2)))
+        across = hop(add(1, inward), ((1, 2), (2, 1)))
+        if chunk == 0:
+            return [hop(add(2, across), ((2, 3), (1, 0)))]
+        return [hop(pick(rounded, 3), ((0, 1), (3, 2))), across]
+
+    def far_exchange(chunk, summed, rounded):
         members = [
             f for f in range(far_count) if (far_quarter <= f < 3 * far_quarter) == (chunk == 1)
         ]
@@ -336,7 +361,8 @@
             return jnp.where(index < far_quarter, index, index - 2 * far_quarter)
 
         kept = lax.dynamic_index_in_dim(summed, place_of(far), 0, keepdims=False)
-        rounded = summed.astype(jnp.bfloat16)
+        if far_count == 4 and chunk == 1:
+            return kept, line_exchange(chunk, summed, rounded)
         arrived = []
         for other in range(1, far_count):
             piece = lax.dynamic_index_in_dim(rounded, place_of(far ^ other), 0, keepdims=False)
@@ -350,14 +376,20 @@
         return kept + sum(value.astype(jnp.float32) for value in arrived)
 
     outer_rows = land(outer_placed)
-    _, outer_summed = near_reduce(outer_rows, OUTER_PARTS)
-    outer_far = [far_exchange(0, value) for value in outer_summed]
+    outer_sent_rows, outer_kept_rows = near_parts(outer_rows)
+    _, outer_arrived = near_exchange(outer_sent_rows, OUTER_PARTS)
     inner_rows = land(inner_placed)
-    _, inner_summed = near_reduce(inner_rows, INNER_PARTS)
-    outer_far, late_rows, inner_summed[0] = lax.optimization_barrier(
-        (outer_far, inner_rows, inner_summed[0])
-    )
-    inner_far = [far_exchange(1, value) for value in inner_summed]
+    inner_sent_rows, inner_kept_rows = near_parts(inner_rows)
+    inner_sent, inner_arrived = near_exchange(inner_sent_rows, INNER_PARTS)
+    outer_arrived[1], _ = lax.optimization_barrier((outer_arrived[1], inner_rows))
+    outer_summed = near_sum(outer_kept_rows, outer_arrived)
+    outer_far = [far_exchange(0, value, value.astype(jnp.bfloat16)) for value in outer_summed]
+    inner_summed = near_sum(inner_kept_rows, inner_arrived)
+    inner_rounded = [value.astype(jnp.bfloat16) for value in inner_summed]
+    outer_far[0], _ = lax.optimization_barrier((outer_far[0], inner_sent))
+    outer_far[1], _ = lax.optimization_barrier((outer_far[1], inner_rounded[0]))
+    late_rows, _ = lax.optimization_barrier((inner_rows, inner_sent))
+    inner_far = [far_exchange(1, *pair) for pair in zip(inner_summed, inner_rounded)]
     grad_parts = [
         jnp.concatenate([far_total(*pair) for pair in pairs], axis=1)
         for pairs in (outer_far, inner_far)

time: 229 us -> 226 us (0.987)
  starting transfers between devices: 73.4 us -> 61.8 us
  Pallas kernels: 31.7 us -> 36.7 us
    ppermute x0 -> x6, waiting for transfers between devices: none -> 16.1 us  [hop(): return lax.ppermute(piece, 'seq', routes)]
    ppermute x12 -> x6, starting transfers between devices: 25.6 us -> 12.8 us  [far_exchange(): arrived.append(lax.ppermute(piece, 'seq', routes))]
    ppermute x0 -> x6, starting transfers between devices: none -> 9.56 us  [hop(): return lax.ppermute(piece, 'seq', routes)]
    ppermute x12 -> x6, waiting for transfers between devices: 7.2 us -> 0.02 us  [far_exchange(): arrived.append(lax.ppermute(piece, 'seq', routes))]
    ppermute x7, waiting for transfers between devices: 36.8 us -> 30.5 us  [swap(): lax.ppermute(value, 'seq', [(i, i ^ bit) for i in range(shard_count)])]
    pallas_call x2, Pallas kernels: 16.7 us -> 20.2 us  [attend_halo(): pl.pallas_call(halo_kernel, out_shape=jax.ShapeDtypeStruct((slot_count, 2...]
    ppermute x7, starting transfers between devices: 6.65 us -> 3.4 us  [swap(): lax.ppermute(value, 'seq', [(i, i ^ bit) for i in range(shard_count)])]
    ppermute x2, starting transfers between devices: 9.17 us -> 6.53 us  [halo(): before = lax.ppermute(pairs[:, row_count - SEG_MAX:], 'seq', up)]
  transfers between devices with their start and end apart: 26 -> 26, of which waited for: 9 -> 7; matrix products, arithmetic and copies ran while one was open for 20% -> 21% of each run, Pallas kernels for 14% -> 16%
where the time goes in v1:
time: 226 us; the launch traced here: 223 us
  waiting for transfers between devices  70.1 us (31%)
  starting transfers between devices  61.8 us (27%)
  Pallas kernels  36.7 us (16%)
  matrix products  33.5 us (15%)
  local copies, waits for them, and re-layouts  12.1 us (5%)
  other arithmetic  7.51 us (3%)
    ppermute x7, waiting for transfers between devices, swap(): lax.ppermute(value, 'seq', [(i, i ^ bit) for i in range(shard_count)])  30.5 us
    all_to_all x2, waiting for transfers between devices, land(): lax.all_to_all(value.reshape(shard_count, capacity, 2 * quarter), 'seq',...  23.5 us
    dot_general x16, matrix products, product(): jnp.einsum('fbt,td->fbd', half, other[:, columns], preferred_element_type...  21.7 us
    pallas_call x2, Pallas kernels, attend_halo(): pl.pallas_call(halo_kernel, out_shape=jax.ShapeDtypeStruct((slot_count, 2...  20.2 us
    all_to_all x2, starting transfers between devices, land(): lax.all_to_all(value.reshape(shard_count, capacity, 2 * quarter), 'seq',...  17.6 us
    pallas_call x2, Pallas kernels, attend_local(): pl.pallas_call(local_kernel, out_shape=(jax.ShapeDtypeStruct((2 * quarter...  16.6 us
    ppermute x6, waiting for transfers between devices, hop(): return lax.ppermute(piece, 'seq', routes)  16.1 us
    ppermute x6, starting transfers between devices, far_exchange(): arrived.append(lax.ppermute(piece, 'seq', routes))  12.8 us
  transfers between devices with their start and end apart: 26, of which 7 were waited for; matrix products, arithmetic and copies ran while one was open for 21% of the time, Pallas kernels for 16%

profile of v1, /device:TPU:10, one launch (start us, length us, event | category | flops | bytes accessed | tf_op | source)
XLA Modules:
  0.0 223.0 jit_solution(13510731776807176749)
XLA Ops:
  5.5 4.5 %collective-permute-start.1 = (bf16[2,512,768]{2,1,0:T(8,128)(2,1)}, bf16[2,512,768]{2,1,0:T(8,128)(2,1)}, u32[]{:S(2)}, u32[]{:S(2)}) collective-permute-start(bf16[2,512,768]{2,1,0:T(8,128)(2,1)} %pad_maximum_fusion), channel_id=1, source_target_pairs={{1,0},{2,1},{3,2},{4,3},{5,4},{6,5},{7,6},{8,7},{9,8},{10,9},{11,1... | collective-permute-start | bytes 4718600 | tf_op jit(solution)/shard_map/ppermute | solution.py:245
  13.0 5.4 %all-to-all-start.1 = ((s32[16,1,64]{2,1,0:T(1,128)}), s32[16,1,64]{2,1,0:T(1,128)S(1)}, u32[]{:S(2)}, u32[]{:S(2)}) async-start(s32[16,1,64]{2,1,0:T(1,128)} %select_n.204), calls=%async_computation.1 | async-start | bytes 16384 | tf_op jit(solution)/shard_map/all_to_all | solution.py:264
  21.8 8.3 %attend_local.2 = (f32[768,512]{1,0:T(8,128)S(1)}, f32[2,6,512]{2,1,0:T(8,128)S(1)}) custom-call(s32[4,6]{1,0:T(4,128)S(1)} %stack.2.bounds, bf16[512,1536]{1,0:T(8,128)(2,1)S(1)} %copy-done, bf16[512,1536]{1,0:T(8,128)(2,1)S(1)} %copy-done, bf16[2,512,1536]{2,1,0:T(8,128)(2,1)} %last_own_ref.3, bf16[2,512,1536]{2,1,0:T(8,128)(2,1)} %last_own_ref.3, ...), custom_call_target="tpu_custom_call" | custom-call | flops 8589934592 | bytes 4194304 | tf_op jit(solution)/shard_map/attend_local/pallas_call | solution.py:142
  31.2 8.3 %attend_local.3 = (f32[768,512]{1,0:T(8,128)S(1)}, f32[2,6,512]{2,1,0:T(8,128)S(1)}) custom-call(s32[4,6]{1,0:T(4,128)S(1)} %stack.2.bounds, bf16[512,1536]{1,0:T(8,128)(2,1)S(1)} %copy-done, bf16[512,1536]{1,0:T(8,128)(2,1)S(1)} %copy-done, bf16[2,512,1536]{2,1,0:T(8,128)(2,1)} %last_own_ref.3, bf16[2,512,1536]{2,1,0:T(8,128)(2,1)} %last_own_ref.3, ...), custom_call_target="tpu_custom_call" | custom-call | flops 8589934592 | bytes 4194304 | tf_op jit(solution)/shard_map/attend_local/pallas_call | solution.py:142
  40.7 4.5 %collective-permute-start.2 = (bf16[2,512,768]{2,1,0:T(8,128)(2,1)}, bf16[2,512,768]{2,1,0:T(8,128)(2,1)}, u32[]{:S(2)}, u32[]{:S(2)}) collective-permute-start(bf16[2,512,768]{2,1,0:T(8,128)(2,1)} %slice.61), channel_id=1, source_target_pairs={{0,1},{1,2},{2,3},{3,4},{4,5},{5,6},{6,7},{7,8},{8,9},{9,10},{10,1... | collective-permute-start | bytes 4718600 | tf_op jit(solution)/shard_map/ppermute | solution.py:244
  47.2 10.1 %attend_halo.2 = bf16[1024,768]{1,0:T(8,128)(2,1)} custom-call(s32[4,6]{1,0:T(4,128)S(1)} %stack.2.bounds, bf16[512,1536]{1,0:T(8,128)(2,1)S(1)} %copy-done, bf16[512,1536]{1,0:T(8,128)(2,1)S(1)} %copy-done, bf16[2,512,768]{2,1,0:T(8,128)(2,1)} %collective-permute-done.before_ref, bf16[2,512,768]{2,1,0:T(8,128)(2,1)} %collective-permute-done.1.after_ref, ...), custom_call_target="tpu_custom_call" | custom-call | flops 17179869184 | bytes 4194304 | tf_op jit(solution)/shard_map/attend_halo/pallas_call | solution.py:169
  57.3 7.8 %all-to-all-start = ((bf16[16,64,768]{2,1,0:T(8,128)(2,1)}), bf16[16,64,768]{2,1,0:T(8,128)(2,1)}, u32[]{:S(2)}, u32[]{:S(2)}) async-start(bf16[16,64,768]{2,1,0:T(8,128)(2,1)} %bitcast.13), calls=%async_computation | async-start | bytes 3145728 | tf_op jit(solution)/shard_map/all_to_all | solution.py:298
  66.5 10.1 %attend_halo.3 = bf16[1024,768]{1,0:T(8,128)(2,1)} custom-call(s32[4,6]{1,0:T(4,128)S(1)} %stack.2.bounds, bf16[512,1536]{1,0:T(8,128)(2,1)S(1)} %copy-done, bf16[512,1536]{1,0:T(8,128)(2,1)S(1)} %copy-done, bf16[2,512,768]{2,1,0:T(8,128)(2,1)} %collective-permute-done.2.before_ref, bf16[2,512,768]{2,1,0:T(8,128)(2,1)} %collective-permute-done.3.after_ref, ...), custom_call_target="tpu_custom_call" | custom-call | flops 17179869184 | bytes 4194304 | tf_op jit(solution)/shard_map/attend_halo/pallas_call | solution.py:169
  76.5 23.5 %all-to-all-done = bf16[16,64,768]{2,1,0:T(8,128)(2,1)} async-done(((bf16[16,64,768]{2,1,0:T(8,128)(2,1)}), bf16[16,64,768]{2,1,0:T(8,128)(2,1)}, u32[]{:S(2)}, u32[]{:S(2)}) %all-to-all-start) | async-done | bytes 1572896 | tf_op jit(solution)/shard_map/all_to_all | solution.py:298
  100.0 9.8 %all-to-all-start.2 = ((bf16[16,64,768]{2,1,0:T(8,128)(2,1)}), bf16[16,64,768]{2,1,0:T(8,128)(2,1)}, u32[]{:S(2)}, u32[]{:S(2)}) async-start(bf16[16,64,768]{2,1,0:T(8,128)(2,1)} %bitcast.15), calls=%async_computation.2 | async-start | bytes 3145728 | tf_op jit(solution)/shard_map/all_to_all | solution.py:298
  109.9 2.7 %fusion.32 = bf16[768,512]{1,0:T(8,128)(2,1)S(1)} fusion(bf16[1024,768]{1,0:T(8,128)(2,1)} %bitcast.14, s32[1024]{0:T(1024)S(1)} %eq.76), kind=kOutput, calls=%fused_computation.48 | convolution fusion | flops 806223872 | bytes 2363392 | tf_op jit(solution)/shard_map/sk,sr->kr/dot_general | solution.py:305
  120.3 2.7 %fusion.7 = bf16[2,96,1536]{2,1,0:T(8,128)(2,1)} fusion(f32[2,96,1536]{2,1,0:T(8,128)S(1)} %fusion.16, bf16[512,3072]{1,0:T(8,128)(2,1)} %collective-permute-done.5, bf16[2,2,96,512]{3,2,1,0:T(8,128)(2,1)S(1)} %bitcast.195, s32[]{:T(128)S(6)} %select_n.209), kind=kOutput, calls=%fused_computation.16 | convolution fusion | flops 302579712 | bytes 3538948 | tf_op jit(solution)/shard_map/fbt,td->fbd/dot_general | solution.py:293
  123.6 19.6 %collective-permute-done.15 = bf16[2,96,1536]{2,1,0:T(8,128)(2,1)S(1)} collective-permute-done((bf16[2,96,1536]{2,1,0:T(8,128)(2,1)S(1)}, bf16[2,96,1536]{2,1,0:T(8,128)(2,1)S(1)}, u32[]{:S(2)}, u32[]{:S(2)}) %collective-permute-start.15) | collective-permute-done | bytes 589856 | tf_op jit(solution)/shard_map/ppermute | solution.py:232
  146.1 2.9 %collective-permute-start.16 = (bf16[96,1536]{1,0:T(8,128)(2,1)}, bf16[96,1536]{1,0:T(8,128)(2,1)}, u32[]{:S(2)}, u32[]{:S(2)}) collective-permute-start(bf16[96,1536]{1,0:T(8,128)(2,1)} %get-tuple-element.62), channel_id=1, source_target_pairs={{4,0},{5,1},{6,2},{7,3},{8,12},{9,13},{10,14},{11,15},{20,16},{21,... | collective-permute-start | bytes 884744 | tf_op jit(solution)/shard_map/ppermute | solution.py:372
  149.0 2.6 %collective-permute-start.17 = (bf16[96,1536]{1,0:T(8,128)(2,1)}, bf16[96,1536]{1,0:T(8,128)(2,1)}, u32[]{:S(2)}, u32[]{:S(2)}) collective-permute-start(bf16[96,1536]{1,0:T(8,128)(2,1)} %get-tuple-element.61), channel_id=1, source_target_pairs={{4,12},{5,13},{6,14},{7,15},{8,0},{9,1},{10,2},{11,3},{20,28},{21,... | collective-permute-start | bytes 884744 | tf_op jit(solution)/shard_map/ppermute | solution.py:372
  153.9 2.5 %fusion.33 = bf16[768,512]{1,0:T(8,128)(2,1)S(1)} fusion(bf16[1024,768]{1,0:T(8,128)(2,1)} %bitcast.16, s32[1024]{0:T(1024)S(1)} %eq.76), kind=kOutput, calls=%fused_computation.49 | convolution fusion | flops 806223872 | bytes 2363392 | tf_op jit(solution)/shard_map/sk,sr->kr/dot_general | solution.py:305
  159.0 2.3 %fusion.114 = (bf16[2,96,1536]{2,1,0:T(8,128)(2,1)S(1)}, f32[2,96,1536]{2,1,0:T(8,128)S(1)}) fusion(bf16[2,96,1536]{2,1,0:T(8,128)(2,1)} %collective-permute-done.19, f32[2,96,1536]{2,1,0:T(8,128)S(1)} %copy-done.4, bf16[512,3072]{1,0:T(8,128)(2,1)} %collective-permute-done.5, bf16[2,2,96,512]{3,2,1,0:T(8,128)(2,1)S(1)} %bitcast.197, s32[]{:T(128)S(6)} %select_n.213), kind=kOutput, calls=%fused_computation.202 | convolution fusion | flops 303169536 | bytes 5308420 | tf_op jit(solution)/shard_map/fbt,td->fbd/dot_general | solution.py:293
  161.5 2.7 %collective-permute-start.20 = (bf16[96,1536]{1,0:T(8,128)(2,1)S(1)}, bf16[96,1536]{1,0:T(8,128)(2,1)S(1)}, u32[]{:S(2)}, u32[]{:S(2)}) collective-permute-start(bf16[96,1536]{1,0:T(8,128)(2,1)S(1)} %get-tuple-element.65), channel_id=1, source_target_pairs={{4,0},{5,1},{6,2},{7,3},{8,12},{9,13},{10,14},{11,15},{20,16},{21,... | collective-permute-start | bytes 884744 | tf_op jit(solution)/shard_map/ppermute | solution.py:372
  169.0 6.6 %add_convert_fusion = bf16[512,3072]{1,0:T(8,128)(2,1)} fusion(bf16[512,3072]{1,0:T(8,128)(2,1)S(1)} %copy-done.12, bf16[1536,3072]{1,0:T(8,128)(2,1)S(1)} %bitcast.205, bf16[384,512]{1,0:T(8,128)(2,1)S(1)} %copy-done.8, bf16[768,512]{1,0:T(8,128)(2,1)S(1)} %fusion.33, bf16[384,512]{1,0:T(8,128)(2,1)S(1)} %copy-done.7), kind=kOutput, calls=%fused_computation | convolution fusion | flops 4841275392 | bytes 17301504 | tf_op jit(solution)/shard_map/kr,kd->rd/dot_general | solution.py:400
  175.5 2.5 %collective-permute-start.21 = (bf16[96,1536]{1,0:T(8,128)(2,1)S(1)}, bf16[96,1536]{1,0:T(8,128)(2,1)S(1)}, u32[]{:S(2)}, u32[]{:S(2)}) collective-permute-start(bf16[96,1536]{1,0:T(8,128)(2,1)S(1)} %get-tuple-element.64), channel_id=1, source_target_pairs={{4,12},{5,13},{6,14},{7,15},{8,0},{9,1},{10,2},{11,3},{20,28},{21,... | collective-permute-start | bytes 884744 | tf_op jit(solution)/shard_map/ppermute | solution.py:372
  180.8 2.2 collective-permute-done.10
  186.3 8.6 %collective-permute-done.6 = bf16[2,96,1536]{2,1,0:T(8,128)(2,1)S(1)} collective-permute-done((bf16[2,96,1536]{2,1,0:T(8,128)(2,1)S(1)}, bf16[2,96,1536]{2,1,0:T(8,128)(2,1)S(1)}, u32[]{:S(2)}, u32[]{:S(2)}) %collective-permute-start.6) | collective-permute-done | bytes 589856 | tf_op jit(solution)/shard_map/ppermute | solution.py:232
  203.2 9.8 %collective-permute-done.8 = bf16[96,1536]{1,0:T(8,128)(2,1)S(1)} collective-permute-done((bf16[96,1536]{1,0:T(8,128)(2,1)S(1)}, bf16[96,1536]{1,0:T(8,128)(2,1)S(1)}, u32[]{:S(2)}, u32[]{:S(2)}) %collective-permute-start.8) | collective-permute-done | bytes 294944 | tf_op jit(solution)/shard_map/ppermute | solution.py:342
  217.6 4.1 %collective-permute-done.9 = bf16[96,1536]{1,0:T(8,128)(2,1)S(1)} collective-permute-done((bf16[96,1536]{1,0:T(8,128)(2,1)S(1)}, bf16[96,1536]{1,0:T(8,128)(2,1)S(1)}, u32[]{:S(2)}, u32[]{:S(2)}) %collective-permute-start.9) | collective-permute-done | bytes 294944 | tf_op jit(solution)/shard_map/ppermute | solution.py:342
  (136 shorter events, 57.6 us)
Async XLA Ops:
  3.5 37.2 %collective-permute-start = (bf16[2,512,768]{2,1,0:T(8,128)(2,1)}, bf16[2,512,768]{2,1,0:T(8,128)(2,1)}, u32[]{:S(2)}, u32[]{:S(2)}) collective-permute-start(bf16[2,512,768]{2,1,0:T(8,128)(2,1)} %pad_maximum_fusion), channel_id=1, source_target_pairs={{0,1},{1,2},{2,3},{3,4},{4,5},{5,6},{6,7},{7,8},{8,9},{9,10},{10,1... | collective-permute-start | bytes 4718600 | tf_op jit(solution)/shard_map/ppermute | solution.py:244
  5.5 35.2 %collective-permute-start.1 = (bf16[2,512,768]{2,1,0:T(8,128)(2,1)}, bf16[2,512,768]{2,1,0:T(8,128)(2,1)}, u32[]{:S(2)}, u32[]{:S(2)}) collective-permute-start(bf16[2,512,768]{2,1,0:T(8,128)(2,1)} %pad_maximum_fusion), channel_id=1, source_target_pairs={{1,0},{2,1},{3,2},{4,3},{5,4},{6,5},{7,6},{8,7},{9,8},{10,9},{11,1... | collective-permute-start | bytes 4718600 | tf_op jit(solution)/shard_map/ppermute | solution.py:245
  13.0 44.3 %all-to-all-start.1 = ((s32[16,1,64]{2,1,0:T(1,128)}), s32[16,1,64]{2,1,0:T(1,128)S(1)}, u32[]{:S(2)}, u32[]{:S(2)}) async-start(s32[16,1,64]{2,1,0:T(1,128)} %select_n.204), calls=%async_computation.1 | async-start | bytes 16384 | tf_op jit(solution)/shard_map/all_to_all | solution.py:264
  40.7 25.7 %collective-permute-start.2 = (bf16[2,512,768]{2,1,0:T(8,128)(2,1)}, bf16[2,512,768]{2,1,0:T(8,128)(2,1)}, u32[]{:S(2)}, u32[]{:S(2)}) collective-permute-start(bf16[2,512,768]{2,1,0:T(8,128)(2,1)} %slice.61), channel_id=1, source_target_pairs={{0,1},{1,2},{2,3},{3,4},{4,5},{5,6},{6,7},{7,8},{8,9},{9,10},{10,1... | collective-permute-start | bytes 4718600 | tf_op jit(solution)/shard_map/ppermute | solution.py:244
  45.2 21.2 %collective-permute-start.3 = (bf16[2,512,768]{2,1,0:T(8,128)(2,1)}, bf16[2,512,768]{2,1,0:T(8,128)(2,1)}, u32[]{:S(2)}, u32[]{:S(2)}) collective-permute-start(bf16[2,512,768]{2,1,0:T(8,128)(2,1)} %slice.61), channel_id=1, source_target_pairs={{1,0},{2,1},{3,2},{4,3},{5,4},{6,5},{7,6},{8,7},{9,8},{10,9},{11,1... | collective-permute-start | bytes 4718600 | tf_op jit(solution)/shard_map/ppermute | solution.py:245
  57.3 42.7 %all-to-all-start = ((bf16[16,64,768]{2,1,0:T(8,128)(2,1)}), bf16[16,64,768]{2,1,0:T(8,128)(2,1)}, u32[]{:S(2)}, u32[]{:S(2)}) async-start(bf16[16,64,768]{2,1,0:T(8,128)(2,1)} %bitcast.13), calls=%async_computation | async-start | bytes 3145728 | tf_op jit(solution)/shard_map/all_to_all | solution.py:298
  65.0 51.3 %collective-permute-start.5 = (bf16[512,3072]{1,0:T(8,128)(2,1)}, bf16[512,3072]{1,0:T(8,128)(2,1)}, u32[]{:S(2)}, u32[]{:S(2)}) collective-permute-start(bf16[512,3072]{1,0:T(8,128)(2,1)} %param.15), channel_id=1, source_target_pairs={{0,1},{1,0},{2,3},{3,2},{4,5},{5,4},{6,7},{7,6},{8,9},{9,8},{10,11... | collective-permute-start | bytes 9437192 | tf_op jit(solution)/shard_map/ppermute | solution.py:232
  100.0 53.8 %all-to-all-start.2 = ((bf16[16,64,768]{2,1,0:T(8,128)(2,1)}), bf16[16,64,768]{2,1,0:T(8,128)(2,1)}, u32[]{:S(2)}, u32[]{:S(2)}) async-start(bf16[16,64,768]{2,1,0:T(8,128)(2,1)} %bitcast.15), calls=%async_computation.2 | async-start | bytes 3145728 | tf_op jit(solution)/shard_map/all_to_all | solution.py:298
  118.3 25.0 %collective-permute-start.15 = (bf16[2,96,1536]{2,1,0:T(8,128)(2,1)S(1)}, bf16[2,96,1536]{2,1,0:T(8,128)(2,1)S(1)}, u32[]{:S(2)}, u32[]{:S(2)}) collective-permute-start(bf16[2,96,1536]{2,1,0:T(8,128)(2,1)S(1)} %fusion.6), channel_id=1, source_target_pairs={{0,2},{1,3},{2,0},{3,1},{4,6},{5,7},{6,4},{7,5},{8,10},{9,11},{10,... | collective-permute-start | bytes 1769480 | tf_op jit(solution)/shard_map/ppermute | solution.py:232
  123.1 35.0 %collective-permute-start.19 = (bf16[2,96,1536]{2,1,0:T(8,128)(2,1)}, bf16[2,96,1536]{2,1,0:T(8,128)(2,1)}, u32[]{:S(2)}, u32[]{:S(2)}) collective-permute-start(bf16[2,96,1536]{2,1,0:T(8,128)(2,1)} %fusion.7), channel_id=1, source_target_pairs={{0,2},{1,3},{2,0},{3,1},{4,6},{5,7},{6,4},{7,5},{8,10},{9,11},{10,... | collective-permute-start | bytes 1769480 | tf_op jit(solution)/shard_map/ppermute | solution.py:232
  146.1 29.4 %collective-permute-start.16 = (bf16[96,1536]{1,0:T(8,128)(2,1)}, bf16[96,1536]{1,0:T(8,128)(2,1)}, u32[]{:S(2)}, u32[]{:S(2)}) collective-permute-start(bf16[96,1536]{1,0:T(8,128)(2,1)} %get-tuple-element.62), channel_id=1, source_target_pairs={{4,0},{5,1},{6,2},{7,3},{8,12},{9,13},{10,14},{11,15},{20,16},{21,... | collective-permute-start | bytes 884744 | tf_op jit(solution)/shard_map/ppermute | solution.py:372
  149.0 29.0 %collective-permute-start.17 = (bf16[96,1536]{1,0:T(8,128)(2,1)}, bf16[96,1536]{1,0:T(8,128)(2,1)}, u32[]{:S(2)}, u32[]{:S(2)}) collective-permute-start(bf16[96,1536]{1,0:T(8,128)(2,1)} %get-tuple-element.61), channel_id=1, source_target_pairs={{4,12},{5,13},{6,14},{7,15},{8,0},{9,1},{10,2},{11,3},{20,28},{21,... | collective-permute-start | bytes 884744 | tf_op jit(solution)/shard_map/ppermute | solution.py:372
  151.6 27.2 %collective-permute-start.18 = (bf16[96,1536]{1,0:T(8,128)(2,1)}, bf16[96,1536]{1,0:T(8,128)(2,1)}, u32[]{:S(2)}, u32[]{:S(2)}) collective-permute-start(bf16[96,1536]{1,0:T(8,128)(2,1)} %get-tuple-element.60), channel_id=1, source_target_pairs={{0,12},{1,13},{2,14},{3,15},{12,0},{13,1},{14,2},{15,3},{16,28},{1... | collective-permute-start | bytes 884744 | tf_op jit(solution)/shard_map/ppermute | solution.py:372
  161.5 36.7 %collective-permute-start.20 = (bf16[96,1536]{1,0:T(8,128)(2,1)S(1)}, bf16[96,1536]{1,0:T(8,128)(2,1)S(1)}, u32[]{:S(2)}, u32[]{:S(2)}) collective-permute-start(bf16[96,1536]{1,0:T(8,128)(2,1)S(1)} %get-tuple-element.65), channel_id=1, source_target_pairs={{4,0},{5,1},{6,2},{7,3},{8,12},{9,13},{10,14},{11,15},{20,16},{21,... | collective-permute-start | bytes 884744 | tf_op jit(solution)/shard_map/ppermute | solution.py:372
  166.8 16.2 %collective-permute-start.10 = (bf16[2,96,1536]{2,1,0:T(8,128)(2,1)S(1)}, bf16[2,96,1536]{2,1,0:T(8,128)(2,1)S(1)}, u32[]{:S(2)}, u32[]{:S(2)}) collective-permute-start(bf16[2,96,1536]{2,1,0:T(8,128)(2,1)S(1)} %fusion.5), channel_id=1, source_target_pairs={{0,2},{1,3},{2,0},{3,1},{4,6},{5,7},{6,4},{7,5},{8,10},{9,11},{10,... | collective-permute-start | bytes 1769480 | tf_op jit(solution)/shard_map/ppermute | solution.py:232
  175.5 23.9 %collective-permute-start.21 = (bf16[96,1536]{1,0:T(8,128)(2,1)S(1)}, bf16[96,1536]{1,0:T(8,128)(2,1)S(1)}, u32[]{:S(2)}, u32[]{:S(2)}) collective-permute-start(bf16[96,1536]{1,0:T(8,128)(2,1)S(1)} %get-tuple-element.64), channel_id=1, source_target_pairs={{4,12},{5,13},{6,14},{7,15},{8,0},{9,1},{10,2},{11,3},{20,28},{21,... | collective-permute-start | bytes 884744 | tf_op jit(solution)/shard_map/ppermute | solution.py:372
  178.1 22.7 %collective-permute-start.22 = (bf16[96,1536]{1,0:T(8,128)(2,1)S(1)}, bf16[96,1536]{1,0:T(8,128)(2,1)S(1)}, u32[]{:S(2)}, u32[]{:S(2)}) collective-permute-start(bf16[96,1536]{1,0:T(8,128)(2,1)S(1)} %get-tuple-element.63), channel_id=1, source_target_pairs={{0,12},{1,13},{2,14},{3,15},{12,0},{13,1},{14,2},{15,3},{16,28},{1... | collective-permute-start | bytes 884744 | tf_op jit(solution)/shard_map/ppermute | solution.py:372
  178.8 16.1 %collective-permute-start.6 = (bf16[2,96,1536]{2,1,0:T(8,128)(2,1)S(1)}, bf16[2,96,1536]{2,1,0:T(8,128)(2,1)S(1)}, u32[]{:S(2)}, u32[]{:S(2)}) collective-permute-start(bf16[2,96,1536]{2,1,0:T(8,128)(2,1)S(1)} %fusion.4), channel_id=1, source_target_pairs={{0,2},{1,3},{2,0},{3,1},{4,6},{5,7},{6,4},{7,5},{8,10},{9,11},{10,... | collective-permute-start | bytes 1769480 | tf_op jit(solution)/shard_map/ppermute | solution.py:232
  185.0 15.9 %collective-permute-start.12 = (bf16[96,1536]{1,0:T(8,128)(2,1)S(1)}, bf16[96,1536]{1,0:T(8,128)(2,1)S(1)}, u32[]{:S(2)}, u32[]{:S(2)}) collective-permute-start(bf16[96,1536]{1,0:T(8,128)(2,1)S(1)} %get-tuple-element.69), channel_id=1, source_target_pairs={{0,4},{1,5},{2,6},{3,7},{12,8},{13,9},{14,10},{15,11},{16,20},{17,... | collective-permute-start | bytes 884744 | tf_op jit(solution)/shard_map/ppermute | solution.py:342
  194.9 20.4 %collective-permute-start.11 = (bf16[96,1536]{1,0:T(8,128)(2,1)S(1)}, bf16[96,1536]{1,0:T(8,128)(2,1)S(1)}, u32[]{:S(2)}, u32[]{:S(2)}) collective-permute-start(bf16[96,1536]{1,0:T(8,128)(2,1)S(1)} %get-tuple-element.68), channel_id=1, source_target_pairs={{0,4},{1,5},{2,6},{3,7},{12,8},{13,9},{14,10},{15,11},{16,20},{17,... | collective-permute-start | bytes 884744 | tf_op jit(solution)/shard_map/ppermute | solution.py:342
  198.1 14.9 %collective-permute-start.8 = (bf16[96,1536]{1,0:T(8,128)(2,1)S(1)}, bf16[96,1536]{1,0:T(8,128)(2,1)S(1)}, u32[]{:S(2)}, u32[]{:S(2)}) collective-permute-start(bf16[96,1536]{1,0:T(8,128)(2,1)S(1)} %get-tuple-element.67), channel_id=1, source_target_pairs={{0,4},{1,5},{2,6},{3,7},{12,8},{13,9},{14,10},{15,11},{16,20},{17,... | collective-permute-start | bytes 884744 | tf_op jit(solution)/shard_map/ppermute | solution.py:342
  199.4 18.2 %collective-permute-start.7 = (bf16[96,1536]{1,0:T(8,128)(2,1)S(1)}, bf16[96,1536]{1,0:T(8,128)(2,1)S(1)}, u32[]{:S(2)}, u32[]{:S(2)}) collective-permute-start(bf16[96,1536]{1,0:T(8,128)(2,1)S(1)} %get-tuple-element.66), channel_id=1, source_target_pairs={{0,4},{1,5},{2,6},{3,7},{12,8},{13,9},{14,10},{15,11},{16,20},{17,... | collective-permute-start | bytes 884744 | tf_op jit(solution)/shard_map/ppermute | solution.py:342
  201.0 14.3 %collective-permute-start.13 = (bf16[96,1536]{1,0:T(8,128)(2,1)S(1)}, bf16[96,1536]{1,0:T(8,128)(2,1)S(1)}, u32[]{:S(2)}, u32[]{:S(2)}) collective-permute-start(bf16[96,1536]{1,0:T(8,128)(2,1)S(1)} %fusion.44), channel_id=1, source_target_pairs={{4,8},{5,9},{6,10},{7,11},{8,4},{9,5},{10,6},{11,7},{20,24},{21,25... | collective-permute-start | bytes 884744 | tf_op jit(solution)/shard_map/ppermute | solution.py:342
  213.1 8.6 %collective-permute-start.9 = (bf16[96,1536]{1,0:T(8,128)(2,1)S(1)}, bf16[96,1536]{1,0:T(8,128)(2,1)S(1)}, u32[]{:S(2)}, u32[]{:S(2)}) collective-permute-start(bf16[96,1536]{1,0:T(8,128)(2,1)S(1)} %fusion.45), channel_id=1, source_target_pairs={{4,8},{5,9},{6,10},{7,11},{8,4},{9,5},{10,6},{11,7},{20,24},{21,25... | collective-permute-start | bytes 884744 | tf_op jit(solution)/shard_map/ppermute | solution.py:342
  (18 other events, 121.5 us)

commit v2 on v1

--- a/solution.py
+++ b/solution.py
@@ -377,18 +377,29 @@
 
     outer_rows = land(outer_placed)
     outer_sent_rows, outer_kept_rows = near_parts(outer_rows)
-    _, outer_arrived = near_exchange(outer_sent_rows, OUTER_PARTS)
+    outer_sent, outer_arrived = near_exchange(outer_sent_rows, OUTER_PARTS)
+    early_rows, _ = lax.optimization_barrier((outer_rows, outer_sent))
+    def project(rows, weights):
+        return jnp.einsum("kr,kd->rd", rows, weights, preferred_element_type=jnp.float32)
+
+    inner_weights = control_proj[quarter : 3 * quarter]
+    early_mixed = (
+        base_hidden.astype(jnp.float32)
+        + project(early_rows[:quarter], control_proj[:quarter])
+        + project(early_rows[quarter:], control_proj[3 * quarter :])
+    )
     inner_rows = land(inner_placed)
     inner_sent_rows, inner_kept_rows = near_parts(inner_rows)
     inner_sent, inner_arrived = near_exchange(inner_sent_rows, INNER_PARTS)
     outer_arrived[1], _ = lax.optimization_barrier((outer_arrived[1], inner_rows))
+    outer_arrived[0], early_mixed = lax.optimization_barrier((outer_arrived[0], early_mixed))
     outer_summed = near_sum(outer_kept_rows, outer_arrived)
     outer_far = [far_exchange(0, value, value.astype(jnp.bfloat16)) for value in outer_summed]
     inner_summed = near_sum(inner_kept_rows, inner_arrived)
     inner_rounded = [value.astype(jnp.bfloat16) for value in inner_summed]
     outer_far[0], _ = lax.optimization_barrier((outer_far[0], inner_sent))
     outer_far[1], _ = lax.optimization_barrier((outer_far[1], inner_rounded[0]))
-    late_rows, _ = lax.optimization_barrier((inner_rows, inner_sent))
+    late_rows, _ = lax.optimization_barrier((inner_rows, inner_rounded[0]))
     inner_far = [far_exchange(1, *pair) for pair in zip(inner_summed, inner_rounded)]
     grad_parts = [
         jnp.concatenate([far_total(*pair) for pair in pairs], axis=1)
@@ -397,13 +408,7 @@
     in_middle = (far >= far_quarter) & (far < 3 * far_quarter)
     proj_grad = jnp.where(in_middle, grad_parts[1], grad_parts[0])
 
-    added = jnp.einsum(
-        "kr,kd->rd",
-        jnp.concatenate([outer_rows[:quarter], late_rows, outer_rows[quarter:]], axis=0),
-        control_proj,
-        preferred_element_type=jnp.float32,
-    )
-    mixed_hidden = (base_hidden.astype(jnp.float32) + added).astype(jnp.bfloat16)
+    mixed_hidden = (early_mixed + project(late_rows, inner_weights)).astype(jnp.bfloat16)
     return (mixed_hidden, proj_grad)
 
 

time: 226 us -> 225 us (level)
  waiting for transfers between devices: 70.1 us -> 60.1 us
  starting transfers between devices: 61.8 us -> 70.1 us
  other arithmetic: 7.51 us -> 11 us
  matrix products: 33.5 us -> 36 us
    ppermute x7, waiting for transfers between devices: 30.5 us -> 23.1 us  [swap(): lax.ppermute(value, 'seq', [(i, i ^ bit) for i in range(shard_count)])]
    ppermute x6, waiting for transfers between devices: 16.1 us -> 9.1 us  [hop(): return lax.ppermute(piece, 'seq', routes)]
    ppermute x2, waiting for transfers between devices: 0.01 us -> 6.89 us  [halo(): after = lax.ppermute(pairs[:, :SEG_MAX], 'seq', down)]
    all_to_all x2, waiting for transfers between devices: 23.5 us -> 18.4 us  [land(): lax.all_to_all(value.reshape(shard_count, capacity, 2 * quarter), 'seq',...]
    pallas_call x2, Pallas kernels: 20.2 us -> 16.7 us  [attend_halo(): pl.pallas_call(halo_kernel, out_shape=jax.ShapeDtypeStruct((slot_count, 2...]
    all_to_all x2, starting transfers between devices: 17.6 us -> 20.7 us  [land(): lax.all_to_all(value.reshape(shard_count, capacity, 2 * quarter), 'seq',...]
    dot_general x1 -> x3, matrix products: 6.57 us -> 9.46 us  [project(): jnp.einsum('kr,kd->rd', rows, weights, preferred_element_type=jnp.float32)]
    convert_element_type x0 -> x1, other arithmetic: none -> 2.59 us  [body(): (early_mixed + project(late_rows, inner_weights)).astype(jnp.bfloat16)]
  transfers between devices with their start and end apart: 26 -> 26, of which waited for: 7 -> 10; matrix products, arithmetic and copies ran while one was open for 21% -> 23% of each run, Pallas kernels for 16% -> 16%
where the time goes in v2:
time: 225 us; the launch traced here: 224 us
  starting transfers between devices  70.1 us (31%)
  waiting for transfers between devices  60.1 us (27%)
  matrix products  36 us (16%)
  Pallas kernels  34.8 us (15%)
  other arithmetic  11 us (5%)
  local copies, waits for them, and re-layouts  10.7 us (5%)
    ppermute x7, waiting for transfers between devices, swap(): lax.ppermute(value, 'seq', [(i, i ^ bit) for i in range(shard_count)])  23.1 us
    dot_general x16, matrix products, product(): jnp.einsum('fbt,td->fbd', half, other[:, columns], preferred_element_type...  21.4 us
    all_to_all x2, starting transfers between devices, land(): lax.all_to_all(value.reshape(shard_count, capacity, 2 * quarter), 'seq',...  20.7 us
    all_to_all x2, waiting for transfers between devices, land(): lax.all_to_all(value.reshape(shard_count, capacity, 2 * quarter), 'seq',...  18.4 us
    pallas_call x2, Pallas kernels, attend_local(): pl.pallas_call(local_kernel, out_shape=(jax.ShapeDtypeStruct((2 * quarter...  18.1 us
    pallas_call x2, Pallas kernels, attend_halo(): pl.pallas_call(halo_kernel, out_shape=jax.ShapeDtypeStruct((slot_count, 2...  16.7 us
    ppermute x6, starting transfers between devices, far_exchange(): arrived.append(lax.ppermute(piece, 'seq', routes))  13 us
    ppermute x6, starting transfers between devices, hop(): return lax.ppermute(piece, 'seq', routes)  12.1 us
  transfers between devices with their start and end apart: 26, of which 10 were waited for; matrix products, arithmetic and copies ran while one was open for 23% of the time, Pallas kernels for 16%

profile of v2, /device:TPU:10, one launch (start us, length us, event | category | flops | bytes accessed | tf_op | source)
XLA Modules:
  0.0 224.0 jit_solution(7313939019632772572)
XLA Ops:
  5.5 4.5 %collective-permute-start.1 = (bf16[2,512,768]{2,1,0:T(8,128)(2,1)}, bf16[2,512,768]{2,1,0:T(8,128)(2,1)}, u32[]{:S(2)}, u32[]{:S(2)}) collective-permute-start(bf16[2,512,768]{2,1,0:T(8,128)(2,1)} %pad_maximum_fusion), channel_id=1, source_target_pairs={{1,0},{2,1},{3,2},{4,3},{5,4},{6,5},{7,6},{8,7},{9,8},{10,9},{11,1... | collective-permute-start | bytes 4718600 | tf_op jit(solution)/shard_map/ppermute | solution.py:245
  13.0 5.4 %all-to-all-start.1 = ((s32[16,1,64]{2,1,0:T(1,128)}), s32[16,1,64]{2,1,0:T(1,128)S(1)}, u32[]{:S(2)}, u32[]{:S(2)}) async-start(s32[16,1,64]{2,1,0:T(1,128)} %select_n.204), calls=%async_computation.1 | async-start | bytes 16384 | tf_op jit(solution)/shard_map/all_to_all | solution.py:264
  21.8 9.1 %attend_local.3 = (f32[768,512]{1,0:T(8,128)S(1)}, f32[2,6,512]{2,1,0:T(8,128)S(1)}) custom-call(s32[4,6]{1,0:T(4,128)S(1)} %stack.2.bounds, bf16[512,1536]{1,0:T(8,128)(2,1)S(1)} %copy-done, bf16[512,1536]{1,0:T(8,128)(2,1)S(1)} %copy-done, bf16[2,512,1536]{2,1,0:T(8,128)(2,1)} %last_own_ref.3, bf16[2,512,1536]{2,1,0:T(8,128)(2,1)} %last_own_ref.3, ...), custom_call_target="tpu_custom_call" | custom-call | flops 8589934592 | bytes 4194304 | tf_op jit(solution)/shard_map/attend_local/pallas_call | solution.py:142
  30.9 9.1 %attend_local.2 = (f32[768,512]{1,0:T(8,128)S(1)}, f32[2,6,512]{2,1,0:T(8,128)S(1)}) custom-call(s32[4,6]{1,0:T(4,128)S(1)} %stack.2.bounds, bf16[512,1536]{1,0:T(8,128)(2,1)S(1)} %copy-done, bf16[512,1536]{1,0:T(8,128)(2,1)S(1)} %copy-done, bf16[2,512,1536]{2,1,0:T(8,128)(2,1)} %last_own_ref.3, bf16[2,512,1536]{2,1,0:T(8,128)(2,1)} %last_own_ref.3, ...), custom_call_target="tpu_custom_call" | custom-call | flops 8589934592 | bytes 4194304 | tf_op jit(solution)/shard_map/attend_local/pallas_call | solution.py:142
  41.1 4.1 %collective-permute-start.5 = (bf16[2,512,768]{2,1,0:T(8,128)(2,1)}, bf16[2,512,768]{2,1,0:T(8,128)(2,1)}, u32[]{:S(2)}, u32[]{:S(2)}) collective-permute-start(bf16[2,512,768]{2,1,0:T(8,128)(2,1)} %slice.70), channel_id=1, source_target_pairs={{0,1},{1,2},{2,3},{3,4},{4,5},{5,6},{6,7},{7,8},{8,9},{9,10},{10,1... | collective-permute-start | bytes 4718600 | tf_op jit(solution)/shard_map/ppermute | solution.py:244
  47.6 8.3 %attend_halo.2 = bf16[1024,768]{1,0:T(8,128)(2,1)} custom-call(s32[4,6]{1,0:T(4,128)S(1)} %stack.2.bounds, bf16[512,1536]{1,0:T(8,128)(2,1)S(1)} %copy-done, bf16[512,1536]{1,0:T(8,128)(2,1)S(1)} %copy-done, bf16[2,512,768]{2,1,0:T(8,128)(2,1)} %collective-permute-done.before_ref, bf16[2,512,768]{2,1,0:T(8,128)(2,1)} %collective-permute-done.1.after_ref, ...), custom_call_target="tpu_custom_call" | custom-call | flops 17179869184 | bytes 4194304 | tf_op jit(solution)/shard_map/attend_halo/pallas_call | solution.py:169
  55.9 7.6 %all-to-all-start = ((bf16[16,64,768]{2,1,0:T(8,128)(2,1)}), bf16[16,64,768]{2,1,0:T(8,128)(2,1)}, u32[]{:S(2)}, u32[]{:S(2)}) async-start(bf16[16,64,768]{2,1,0:T(8,128)(2,1)} %bitcast.13), calls=%async_computation | async-start | bytes 3145728 | tf_op jit(solution)/shard_map/all_to_all | solution.py:298
  65.0 6.9 %collective-permute-done.6.after_ref = bf16[2,512,768]{2,1,0:T(8,128)(2,1)} collective-permute-done((bf16[2,512,768]{2,1,0:T(8,128)(2,1)}, bf16[2,512,768]{2,1,0:T(8,128)(2,1)}, u32[]{:S(2)}, u32[]{:S(2)}) %collective-permute-start.6) | collective-permute-done | bytes 1572896 | tf_op jit(solution)/shard_map/ppermute | solution.py:245
  71.8 8.3 %attend_halo.3 = bf16[1024,768]{1,0:T(8,128)(2,1)} custom-call(s32[4,6]{1,0:T(4,128)S(1)} %stack.2.bounds, bf16[512,1536]{1,0:T(8,128)(2,1)S(1)} %copy-done, bf16[512,1536]{1,0:T(8,128)(2,1)S(1)} %copy-done, bf16[2,512,768]{2,1,0:T(8,128)(2,1)} %collective-permute-done.5.before_ref, bf16[2,512,768]{2,1,0:T(8,128)(2,1)} %collective-permute-done.6.after_ref, ...), custom_call_target="tpu_custom_call" | custom-call | flops 17179869184 | bytes 4194304 | tf_op jit(solution)/shard_map/attend_halo/pallas_call | solution.py:169
  80.2 18.4 %all-to-all-done = bf16[16,64,768]{2,1,0:T(8,128)(2,1)} async-done(((bf16[16,64,768]{2,1,0:T(8,128)(2,1)}), bf16[16,64,768]{2,1,0:T(8,128)(2,1)}, u32[]{:S(2)}, u32[]{:S(2)}) %all-to-all-start) | async-done | bytes 1572896 | tf_op jit(solution)/shard_map/all_to_all | solution.py:298
  98.6 13.1 %all-to-all-start.2 = ((bf16[16,64,768]{2,1,0:T(8,128)(2,1)}), bf16[16,64,768]{2,1,0:T(8,128)(2,1)}, u32[]{:S(2)}, u32[]{:S(2)}) async-start(bf16[16,64,768]{2,1,0:T(8,128)(2,1)} %bitcast.25), calls=%async_computation.2 | async-start | bytes 3145728 | tf_op jit(solution)/shard_map/all_to_all | solution.py:298
  111.6 2.7 %fusion.32 = bf16[768,512]{1,0:T(8,128)(2,1)S(1)} fusion(bf16[1024,768]{1,0:T(8,128)(2,1)} %bitcast.14, s32[1024]{0:T(1024)S(1)} %eq.76), kind=kOutput, calls=%fused_computation.49 | convolution fusion | flops 806223872 | bytes 2363392 | tf_op jit(solution)/shard_map/sk,sr->kr/dot_general | solution.py:305
  121.1 2.7 %fusion.7 = bf16[2,96,1536]{2,1,0:T(8,128)(2,1)} fusion(f32[2,96,1536]{2,1,0:T(8,128)S(1)} %fusion.22, bf16[512,3072]{1,0:T(8,128)(2,1)} %collective-permute-done.3, bf16[2,2,96,512]{3,2,1,0:T(8,128)(2,1)S(1)} %bitcast.202, s32[]{:T(128)S(6)} %select_n.209), kind=kOutput, calls=%fused_computation.17 | convolution fusion | flops 302579712 | bytes 3538948 | tf_op jit(solution)/shard_map/fbt,td->fbd/dot_general | solution.py:293
  126.3 4.9 %add_add_fusion = f32[512,3072]{1,0:T(8,128)} fusion(f32[512,3072]{1,0:T(8,128)S(1)} %fusion.11, bf16[512,3072]{1,0:T(8,128)(2,1)S(1)} %copy-done.5, bf16[1536,3072]{1,0:T(8,128)(2,1)S(1)} %bitcast.184, bf16[768,512]{1,0:T(8,128)(2,1)S(1)} %fusion.32), kind=kOutput, calls=%fused_computation.1 | convolution fusion | flops 1212678144 | bytes 18481152 | tf_op jit(solution)/shard_map/kr,kd->rd/dot_general | solution.py:383
  131.2 13.0 %collective-permute-done.4 = bf16[2,96,1536]{2,1,0:T(8,128)(2,1)S(1)} collective-permute-done((bf16[2,96,1536]{2,1,0:T(8,128)(2,1)S(1)}, bf16[2,96,1536]{2,1,0:T(8,128)(2,1)S(1)}, u32[]{:S(2)}, u32[]{:S(2)}) %collective-permute-start.4) | collective-permute-done | bytes 589856 | tf_op jit(solution)/shard_map/ppermute | solution.py:232
  147.1 3.6 %collective-permute-start.16 = (bf16[96,1536]{1,0:T(8,128)(2,1)}, bf16[96,1536]{1,0:T(8,128)(2,1)}, u32[]{:S(2)}, u32[]{:S(2)}) collective-permute-start(bf16[96,1536]{1,0:T(8,128)(2,1)} %get-tuple-element.66), channel_id=1, source_target_pairs={{4,0},{5,1},{6,2},{7,3},{8,12},{9,13},{10,14},{11,15},{20,16},{21,... | collective-permute-start | bytes 884744 | tf_op jit(solution)/shard_map/ppermute | solution.py:372
  170.4 3.7 %collective-permute-start.21 = (bf16[96,1536]{1,0:T(8,128)(2,1)S(1)}, bf16[96,1536]{1,0:T(8,128)(2,1)S(1)}, u32[]{:S(2)}, u32[]{:S(2)}) collective-permute-start(bf16[96,1536]{1,0:T(8,128)(2,1)S(1)} %get-tuple-element.68), channel_id=1, source_target_pairs={{4,12},{5,13},{6,14},{7,15},{8,0},{9,1},{10,2},{11,3},{20,28},{21,... | collective-permute-start | bytes 884744 | tf_op jit(solution)/shard_map/ppermute | solution.py:372
  178.2 4.9 %collective-permute-done.8 = bf16[2,96,1536]{2,1,0:T(8,128)(2,1)S(1)} collective-permute-done((bf16[2,96,1536]{2,1,0:T(8,128)(2,1)S(1)}, bf16[2,96,1536]{2,1,0:T(8,128)(2,1)S(1)}, u32[]{:S(2)}, u32[]{:S(2)}) %collective-permute-start.8) | collective-permute-done | bytes 589856 | tf_op jit(solution)/shard_map/ppermute | solution.py:232
  190.1 5.2 %collective-permute-done.12 = bf16[2,96,1536]{2,1,0:T(8,128)(2,1)S(1)} collective-permute-done((bf16[2,96,1536]{2,1,0:T(8,128)(2,1)S(1)}, bf16[2,96,1536]{2,1,0:T(8,128)(2,1)S(1)}, u32[]{:S(2)}, u32[]{:S(2)}) %collective-permute-start.12) | collective-permute-done | bytes 589856 | tf_op jit(solution)/shard_map/ppermute | solution.py:232
  200.3 2.7 %fusion = f32[512,3072]{1,0:T(8,128)S(1)} fusion(bf16[768,512]{1,0:T(8,128)(2,1)S(1)} %fusion.33, bf16[1536,3072]{1,0:T(8,128)(2,1)S(1)} %bitcast.186), kind=kOutput, calls=%fused_computation.2 | convolution fusion | flops 2415919104 | bytes 11796480 | tf_op jit(solution)/shard_map/kr,kd->rd/dot_general | solution.py:383
  205.9 3.7 %collective-permute-start.11 = (bf16[96,1536]{1,0:T(8,128)(2,1)S(1)}, bf16[96,1536]{1,0:T(8,128)(2,1)S(1)}, u32[]{:S(2)}, u32[]{:S(2)}) collective-permute-start(bf16[96,1536]{1,0:T(8,128)(2,1)S(1)} %fusion.45), channel_id=1, source_target_pairs={{4,8},{5,9},{6,10},{7,11},{8,4},{9,5},{10,6},{11,7},{20,24},{21,25... | collective-permute-start | bytes 884744 | tf_op jit(solution)/shard_map/ppermute | solution.py:342
  211.7 2.9 %collective-permute-start.15 = (bf16[96,1536]{1,0:T(8,128)(2,1)S(1)}, bf16[96,1536]{1,0:T(8,128)(2,1)S(1)}, u32[]{:S(2)}, u32[]{:S(2)}) collective-permute-start(bf16[96,1536]{1,0:T(8,128)(2,1)S(1)} %fusion.44), channel_id=1, source_target_pairs={{4,8},{5,9},{6,10},{7,11},{8,4},{9,5},{10,6},{11,7},{20,24},{21,25... | collective-permute-start | bytes 884744 | tf_op jit(solution)/shard_map/ppermute | solution.py:342
  214.6 3.1 %collective-permute-done.11 = bf16[96,1536]{1,0:T(8,128)(2,1)S(1)} collective-permute-done((bf16[96,1536]{1,0:T(8,128)(2,1)S(1)}, bf16[96,1536]{1,0:T(8,128)(2,1)S(1)}, u32[]{:S(2)}, u32[]{:S(2)}) %collective-permute-start.11) | collective-permute-done | bytes 294944 | tf_op jit(solution)/shard_map/ppermute | solution.py:342
  217.8 4.9 %collective-permute-done.15 = bf16[96,1536]{1,0:T(8,128)(2,1)S(1)} collective-permute-done((bf16[96,1536]{1,0:T(8,128)(2,1)S(1)}, bf16[96,1536]{1,0:T(8,128)(2,1)S(1)}, u32[]{:S(2)}, u32[]{:S(2)}) %collective-permute-start.15) | collective-permute-done | bytes 294944 | tf_op jit(solution)/shard_map/ppermute | solution.py:342
  (148 shorter events, 69.8 us)
Async XLA Ops:
  3.5 37.6 %collective-permute-start = (bf16[2,512,768]{2,1,0:T(8,128)(2,1)}, bf16[2,512,768]{2,1,0:T(8,128)(2,1)}, u32[]{:S(2)}, u32[]{:S(2)}) collective-permute-start(bf16[2,512,768]{2,1,0:T(8,128)(2,1)} %pad_maximum_fusion), channel_id=1, source_target_pairs={{0,1},{1,2},{2,3},{3,4},{4,5},{5,6},{6,7},{7,8},{8,9},{9,10},{10,1... | collective-permute-start | bytes 4718600 | tf_op jit(solution)/shard_map/ppermute | solution.py:244
  5.5 35.6 %collective-permute-start.1 = (bf16[2,512,768]{2,1,0:T(8,128)(2,1)}, bf16[2,512,768]{2,1,0:T(8,128)(2,1)}, u32[]{:S(2)}, u32[]{:S(2)}) collective-permute-start(bf16[2,512,768]{2,1,0:T(8,128)(2,1)} %pad_maximum_fusion), channel_id=1, source_target_pairs={{1,0},{2,1},{3,2},{4,3},{5,4},{6,5},{7,6},{8,7},{9,8},{10,9},{11,1... | collective-permute-start | bytes 4718600 | tf_op jit(solution)/shard_map/ppermute | solution.py:245
  13.0 43.0 %all-to-all-start.1 = ((s32[16,1,64]{2,1,0:T(1,128)}), s32[16,1,64]{2,1,0:T(1,128)S(1)}, u32[]{:S(2)}, u32[]{:S(2)}) async-start(s32[16,1,64]{2,1,0:T(1,128)} %select_n.204), calls=%async_computation.1 | async-start | bytes 16384 | tf_op jit(solution)/shard_map/all_to_all | solution.py:264
  41.1 23.8 %collective-permute-start.5 = (bf16[2,512,768]{2,1,0:T(8,128)(2,1)}, bf16[2,512,768]{2,1,0:T(8,128)(2,1)}, u32[]{:S(2)}, u32[]{:S(2)}) collective-permute-start(bf16[2,512,768]{2,1,0:T(8,128)(2,1)} %slice.70), channel_id=1, source_target_pairs={{0,1},{1,2},{2,3},{3,4},{4,5},{5,6},{6,7},{7,8},{8,9},{9,10},{10,1... | collective-permute-start | bytes 4718600 | tf_op jit(solution)/shard_map/ppermute | solution.py:244
  45.2 26.6 %collective-permute-start.6 = (bf16[2,512,768]{2,1,0:T(8,128)(2,1)}, bf16[2,512,768]{2,1,0:T(8,128)(2,1)}, u32[]{:S(2)}, u32[]{:S(2)}) collective-permute-start(bf16[2,512,768]{2,1,0:T(8,128)(2,1)} %slice.70), channel_id=1, source_target_pairs={{1,0},{2,1},{3,2},{4,3},{5,4},{6,5},{7,6},{8,7},{9,8},{10,9},{11,1... | collective-permute-start | bytes 4718600 | tf_op jit(solution)/shard_map/ppermute | solution.py:245
  55.9 42.6 %all-to-all-start = ((bf16[16,64,768]{2,1,0:T(8,128)(2,1)}), bf16[16,64,768]{2,1,0:T(8,128)(2,1)}, u32[]{:S(2)}, u32[]{:S(2)}) async-start(bf16[16,64,768]{2,1,0:T(8,128)(2,1)} %bitcast.13), calls=%async_computation | async-start | bytes 3145728 | tf_op jit(solution)/shard_map/all_to_all | solution.py:298
  63.5 54.1 %collective-permute-start.3 = (bf16[512,3072]{1,0:T(8,128)(2,1)}, bf16[512,3072]{1,0:T(8,128)(2,1)}, u32[]{:S(2)}, u32[]{:S(2)}) collective-permute-start(bf16[512,3072]{1,0:T(8,128)(2,1)} %param.15), channel_id=1, source_target_pairs={{0,1},{1,0},{2,3},{3,2},{4,5},{5,4},{6,7},{7,6},{8,9},{9,8},{10,11... | collective-permute-start | bytes 9437192 | tf_op jit(solution)/shard_map/ppermute | solution.py:232
  98.6 56.5 %all-to-all-start.2 = ((bf16[16,64,768]{2,1,0:T(8,128)(2,1)}), bf16[16,64,768]{2,1,0:T(8,128)(2,1)}, u32[]{:S(2)}, u32[]{:S(2)}) async-start(bf16[16,64,768]{2,1,0:T(8,128)(2,1)} %bitcast.25), calls=%async_computation.2 | async-start | bytes 3145728 | tf_op jit(solution)/shard_map/all_to_all | solution.py:298
  119.6 24.6 %collective-permute-start.4 = (bf16[2,96,1536]{2,1,0:T(8,128)(2,1)S(1)}, bf16[2,96,1536]{2,1,0:T(8,128)(2,1)S(1)}, u32[]{:S(2)}, u32[]{:S(2)}) collective-permute-start(bf16[2,96,1536]{2,1,0:T(8,128)(2,1)S(1)} %fusion.6), channel_id=1, source_target_pairs={{0,2},{1,3},{2,0},{3,1},{4,6},{5,7},{6,4},{7,5},{8,10},{9,11},{10,... | collective-permute-start | bytes 1769480 | tf_op jit(solution)/shard_map/ppermute | solution.py:232
  123.9 35.4 %collective-permute-start.19 = (bf16[2,96,1536]{2,1,0:T(8,128)(2,1)}, bf16[2,96,1536]{2,1,0:T(8,128)(2,1)}, u32[]{:S(2)}, u32[]{:S(2)}) collective-permute-start(bf16[2,96,1536]{2,1,0:T(8,128)(2,1)} %fusion.7), channel_id=1, source_target_pairs={{0,2},{1,3},{2,0},{3,1},{4,6},{5,7},{6,4},{7,5},{8,10},{9,11},{10,... | collective-permute-start | bytes 1769480 | tf_op jit(solution)/shard_map/ppermute | solution.py:232
  147.1 23.3 %collective-permute-start.16 = (bf16[96,1536]{1,0:T(8,128)(2,1)}, bf16[96,1536]{1,0:T(8,128)(2,1)}, u32[]{:S(2)}, u32[]{:S(2)}) collective-permute-start(bf16[96,1536]{1,0:T(8,128)(2,1)} %get-tuple-element.66), channel_id=1, source_target_pairs={{4,0},{5,1},{6,2},{7,3},{8,12},{9,13},{10,14},{11,15},{20,16},{21,... | collective-permute-start | bytes 884744 | tf_op jit(solution)/shard_map/ppermute | solution.py:372
  150.8 23.4 %collective-permute-start.17 = (bf16[96,1536]{1,0:T(8,128)(2,1)}, bf16[96,1536]{1,0:T(8,128)(2,1)}, u32[]{:S(2)}, u32[]{:S(2)}) collective-permute-start(bf16[96,1536]{1,0:T(8,128)(2,1)} %get-tuple-element.65), channel_id=1, source_target_pairs={{4,12},{5,13},{6,14},{7,15},{8,0},{9,1},{10,2},{11,3},{20,28},{21,... | collective-permute-start | bytes 884744 | tf_op jit(solution)/shard_map/ppermute | solution.py:372
  152.8 22.3 %collective-permute-start.18 = (bf16[96,1536]{1,0:T(8,128)(2,1)}, bf16[96,1536]{1,0:T(8,128)(2,1)}, u32[]{:S(2)}, u32[]{:S(2)}) collective-permute-start(bf16[96,1536]{1,0:T(8,128)(2,1)} %get-tuple-element.64), channel_id=1, source_target_pairs={{0,12},{1,13},{2,14},{3,15},{12,0},{13,1},{14,2},{15,3},{16,28},{1... | collective-permute-start | bytes 884744 | tf_op jit(solution)/shard_map/ppermute | solution.py:372
  162.1 25.3 %collective-permute-start.20 = (bf16[96,1536]{1,0:T(8,128)(2,1)S(1)}, bf16[96,1536]{1,0:T(8,128)(2,1)S(1)}, u32[]{:S(2)}, u32[]{:S(2)}) collective-permute-start(bf16[96,1536]{1,0:T(8,128)(2,1)S(1)} %get-tuple-element.69), channel_id=1, source_target_pairs={{4,0},{5,1},{6,2},{7,3},{8,12},{9,13},{10,14},{11,15},{20,16},{21,... | collective-permute-start | bytes 884744 | tf_op jit(solution)/shard_map/ppermute | solution.py:372
  166.9 16.2 %collective-permute-start.8 = (bf16[2,96,1536]{2,1,0:T(8,128)(2,1)S(1)}, bf16[2,96,1536]{2,1,0:T(8,128)(2,1)S(1)}, u32[]{:S(2)}, u32[]{:S(2)}) collective-permute-start(bf16[2,96,1536]{2,1,0:T(8,128)(2,1)S(1)} %fusion.8), channel_id=1, source_target_pairs={{0,2},{1,3},{2,0},{3,1},{4,6},{5,7},{6,4},{7,5},{8,10},{9,11},{10,... | collective-permute-start | bytes 1769480 | tf_op jit(solution)/shard_map/ppermute | solution.py:232
  170.4 17.0 %collective-permute-start.21 = (bf16[96,1536]{1,0:T(8,128)(2,1)S(1)}, bf16[96,1536]{1,0:T(8,128)(2,1)S(1)}, u32[]{:S(2)}, u32[]{:S(2)}) collective-permute-start(bf16[96,1536]{1,0:T(8,128)(2,1)S(1)} %get-tuple-element.68), channel_id=1, source_target_pairs={{4,12},{5,13},{6,14},{7,15},{8,0},{9,1},{10,2},{11,3},{20,28},{21,... | collective-permute-start | bytes 884744 | tf_op jit(solution)/shard_map/ppermute | solution.py:372
  174.2 13.3 %collective-permute-start.22 = (bf16[96,1536]{1,0:T(8,128)(2,1)S(1)}, bf16[96,1536]{1,0:T(8,128)(2,1)S(1)}, u32[]{:S(2)}, u32[]{:S(2)}) collective-permute-start(bf16[96,1536]{1,0:T(8,128)(2,1)S(1)} %get-tuple-element.67), channel_id=1, source_target_pairs={{0,12},{1,13},{2,14},{3,15},{12,0},{13,1},{14,2},{15,3},{16,28},{1... | collective-permute-start | bytes 884744 | tf_op jit(solution)/shard_map/ppermute | solution.py:372
  175.1 20.2 %collective-permute-start.12 = (bf16[2,96,1536]{2,1,0:T(8,128)(2,1)S(1)}, bf16[2,96,1536]{2,1,0:T(8,128)(2,1)S(1)}, u32[]{:S(2)}, u32[]{:S(2)}) collective-permute-start(bf16[2,96,1536]{2,1,0:T(8,128)(2,1)S(1)} %fusion.9), channel_id=1, source_target_pairs={{0,2},{1,3},{2,0},{3,1},{4,6},{5,7},{6,4},{7,5},{8,10},{9,11},{10,... | collective-permute-start | bytes 1769480 | tf_op jit(solution)/shard_map/ppermute | solution.py:232
  187.5 18.3 %collective-permute-start.10 = (bf16[96,1536]{1,0:T(8,128)(2,1)S(1)}, bf16[96,1536]{1,0:T(8,128)(2,1)S(1)}, u32[]{:S(2)}, u32[]{:S(2)}) collective-permute-start(bf16[96,1536]{1,0:T(8,128)(2,1)S(1)} %get-tuple-element.71), channel_id=1, source_target_pairs={{0,4},{1,5},{2,6},{3,7},{12,8},{13,9},{14,10},{15,11},{16,20},{17,... | collective-permute-start | bytes 884744 | tf_op jit(solution)/shard_map/ppermute | solution.py:342
  188.8 25.8 %collective-permute-start.9 = (bf16[96,1536]{1,0:T(8,128)(2,1)S(1)}, bf16[96,1536]{1,0:T(8,128)(2,1)S(1)}, u32[]{:S(2)}, u32[]{:S(2)}) collective-permute-start(bf16[96,1536]{1,0:T(8,128)(2,1)S(1)} %get-tuple-element.70), channel_id=1, source_target_pairs={{0,4},{1,5},{2,6},{3,7},{12,8},{13,9},{14,10},{15,11},{16,20},{17,... | collective-permute-start | bytes 884744 | tf_op jit(solution)/shard_map/ppermute | solution.py:342
  197.3 13.4 %collective-permute-start.14 = (bf16[96,1536]{1,0:T(8,128)(2,1)S(1)}, bf16[96,1536]{1,0:T(8,128)(2,1)}, u32[]{:S(2)}, u32[]{:S(2)}) collective-permute-start(bf16[96,1536]{1,0:T(8,128)(2,1)S(1)} %get-tuple-element.73), channel_id=1, source_target_pairs={{0,4},{1,5},{2,6},{3,7},{12,8},{13,9},{14,10},{15,11},{16,20},{17,... | collective-permute-start | bytes 884744 | tf_op jit(solution)/shard_map/ppermute | solution.py:342
  198.9 19.0 %collective-permute-start.13 = (bf16[96,1536]{1,0:T(8,128)(2,1)S(1)}, bf16[96,1536]{1,0:T(8,128)(2,1)S(1)}, u32[]{:S(2)}, u32[]{:S(2)}) collective-permute-start(bf16[96,1536]{1,0:T(8,128)(2,1)S(1)} %get-tuple-element.72), channel_id=1, source_target_pairs={{0,4},{1,5},{2,6},{3,7},{12,8},{13,9},{14,10},{15,11},{16,20},{17,... | collective-permute-start | bytes 884744 | tf_op jit(solution)/shard_map/ppermute | solution.py:342
  205.9 11.8 %collective-permute-start.11 = (bf16[96,1536]{1,0:T(8,128)(2,1)S(1)}, bf16[96,1536]{1,0:T(8,128)(2,1)S(1)}, u32[]{:S(2)}, u32[]{:S(2)}) collective-permute-start(bf16[96,1536]{1,0:T(8,128)(2,1)S(1)} %fusion.45), channel_id=1, source_target_pairs={{4,8},{5,9},{6,10},{7,11},{8,4},{9,5},{10,6},{11,7},{20,24},{21,25... | collective-permute-start | bytes 884744 | tf_op jit(solution)/shard_map/ppermute | solution.py:342
  211.7 11.0 %collective-permute-start.15 = (bf16[96,1536]{1,0:T(8,128)(2,1)S(1)}, bf16[96,1536]{1,0:T(8,128)(2,1)S(1)}, u32[]{:S(2)}, u32[]{:S(2)}) collective-permute-start(bf16[96,1536]{1,0:T(8,128)(2,1)S(1)} %fusion.44), channel_id=1, source_target_pairs={{4,8},{5,9},{6,10},{7,11},{8,4},{9,5},{10,6},{11,7},{20,24},{21,25... | collective-permute-start | bytes 884744 | tf_op jit(solution)/shard_map/ppermute | solution.py:342
  (22 other events, 227.9 us)

commit v3 on v2

--- a/solution.py
+++ b/solution.py
@@ -153,7 +153,7 @@
             + [query_lanes(1), whole(row_count, 1)],
             out_specs=[query_lanes(2 * quarter), query_lanes(2, head_count)],
         ),
-        compiler_params=pltpu.CompilerParams(vmem_limit_bytes=48 << 20),
+        compiler_params=pltpu.CompilerParams(vmem_limit_bytes=24 << 20),
         cost_estimate=pl.CostEstimate(
             flops=LOCAL_FLOPS_HINT, transcendentals=1 << 20, bytes_accessed=1 << 22
         ),
@@ -185,7 +185,7 @@
             out_specs=whole(slot_count, 2 * quarter),
             scratch_shapes=[pltpu.VMEM((row_count, 2 * quarter), jnp.bfloat16)],
         ),
-        compiler_params=pltpu.CompilerParams(vmem_limit_bytes=48 << 20),
+        compiler_params=pltpu.CompilerParams(vmem_limit_bytes=24 << 20),
         cost_estimate=pl.CostEstimate(
             flops=HALO_FLOPS_HINT, transcendentals=1 << 20, bytes_accessed=1 << 22
         ),

time: 225 us -> 228 us (1.013); the launches traced: 224 us -> 224 us
  local copies, waits for them, and re-layouts: 10.7 us -> 15.9 us
  starting transfers between devices: 70.1 us -> 65.8 us
  Pallas kernels: 34.8 us -> 32.5 us
    unnamed x40 -> x52, local copies, waits for them, and re-layouts: 2.06 us -> 5.85 us
    all_to_all x2, starting transfers between devices: 20.7 us -> 17.9 us  [land(): lax.all_to_all(value.reshape(shard_count, capacity, 2 * quarter), 'seq',...]
    pallas_call x2, Pallas kernels: 18.1 us -> 15.7 us  [attend_local(): pl.pallas_call(local_kernel, out_shape=(jax.ShapeDtypeStruct((2 * quarter...]
    all_to_all x2, waiting for transfers between devices: 18.4 us -> 16.1 us  [land(): lax.all_to_all(value.reshape(shard_count, capacity, 2 * quarter), 'seq',...]
    ppermute x7, waiting for transfers between devices: 23.1 us -> 25.4 us  [swap(): lax.ppermute(value, 'seq', [(i, i ^ bit) for i in range(shard_count)])]
  transfers between devices with their start and end apart: 26 -> 26, of which waited for: 10 -> 9; matrix products, arithmetic and copies ran while one was open for 23% -> 24% of each run, Pallas kernels for 16% -> 14%
where the time goes in v3:
time: 228 us; the launch traced here: 224 us
  starting transfers between devices  65.8 us (29%)
  waiting for transfers between devices  60.5 us (27%)
  matrix products  36.3 us (16%)
  Pallas kernels  32.5 us (14%)
  local copies, waits for them, and re-layouts  15.9 us (7%)
  other arithmetic  11.9 us (5%)
    ppermute x7, waiting for transfers between devices, swap(): lax.ppermute(value, 'seq', [(i, i ^ bit) for i in range(shard_count)])  25.4 us
    dot_general x16, matrix products, product(): jnp.einsum('fbt,td->fbd', half, other[:, columns], preferred_element_type...  21.7 us
    all_to_all x2, starting transfers between devices, land(): lax.all_to_all(value.reshape(shard_count, capacity, 2 * quarter), 'seq',...  17.9 us
    pallas_call x2, Pallas kernels, attend_halo(): pl.pallas_call(halo_kernel, out_shape=jax.ShapeDtypeStruct((slot_count, 2...  16.8 us
    all_to_all x2, waiting for transfers between devices, land(): lax.all_to_all(value.reshape(shard_count, capacity, 2 * quarter), 'seq',...  16.1 us
    pallas_call x2, Pallas kernels, attend_local(): pl.pallas_call(local_kernel, out_shape=(jax.ShapeDtypeStruct((2 * quarter...  15.7 us
    ppermute x6, starting transfers between devices, far_exchange(): arrived.append(lax.ppermute(piece, 'seq', routes))  14.6 us
    ppermute x6, starting transfers between devices, hop(): return lax.ppermute(piece, 'seq', routes)  11 us
  transfers between devices with their start and end apart: 26, of which 9 were waited for; matrix products, arithmetic and copies ran while one was open for 24% of the time, Pallas kernels for 14%

profile of v3, /device:TPU:10, one launch (start us, length us, event | category | flops | bytes accessed | tf_op | source)
XLA Modules:
  0.0 224.3 jit_solution(15156230231634033027)
XLA Ops:
  5.5 4.5 %collective-permute-start.1 = (bf16[2,512,768]{2,1,0:T(8,128)(2,1)}, bf16[2,512,768]{2,1,0:T(8,128)(2,1)}, u32[]{:S(2)}, u32[]{:S(2)}) collective-permute-start(bf16[2,512,768]{2,1,0:T(8,128)(2,1)} %pad_maximum_fusion), channel_id=1, source_target_pairs={{1,0},{2,1},{3,2},{4,3},{5,4},{6,5},{7,6},{8,7},{9,8},{10,9},{11,1... | collective-permute-start | bytes 4718600 | tf_op jit(solution)/shard_map/ppermute | solution.py:245
  13.0 5.4 %all-to-all-start.1 = ((s32[16,1,64]{2,1,0:T(1,128)}), s32[16,1,64]{2,1,0:T(1,128)S(1)}, u32[]{:S(2)}, u32[]{:S(2)}) async-start(s32[16,1,64]{2,1,0:T(1,128)} %select_n.204), calls=%async_computation.1 | async-start | bytes 16384 | tf_op jit(solution)/shard_map/all_to_all | solution.py:264
  26.6 7.9 %attend_local.3 = (f32[768,512]{1,0:T(8,128)S(1)}, f32[2,6,512]{2,1,0:T(8,128)S(1)}) custom-call(s32[4,6]{1,0:T(4,128)S(1)} %stack.2.bounds, bf16[512,1536]{1,0:T(8,128)(2,1)S(1)} %copy-done.6, bf16[512,1536]{1,0:T(8,128)(2,1)S(1)} %copy-done.6, bf16[2,512,1536]{2,1,0:T(8,128)(2,1)S(1)} %copy-done, bf16[2,512,1536]{2,1,0:T(8,128)(2,1)S(1)} %copy-done, ...), custom_call_target="tpu_custom_call" | custom-call | flops 8589934592 | bytes 4194304 | tf_op jit(solution)/shard_map/attend_local/pallas_call | solution.py:142
  35.6 7.9 %attend_local.2 = (f32[768,512]{1,0:T(8,128)S(1)}, f32[2,6,512]{2,1,0:T(8,128)S(1)}) custom-call(s32[4,6]{1,0:T(4,128)S(1)} %stack.2.bounds, bf16[512,1536]{1,0:T(8,128)(2,1)S(1)} %copy-done.6, bf16[512,1536]{1,0:T(8,128)(2,1)S(1)} %copy-done.6, bf16[2,512,1536]{2,1,0:T(8,128)(2,1)S(1)} %copy-done, bf16[2,512,1536]{2,1,0:T(8,128)(2,1)S(1)} %copy-done, ...), custom_call_target="tpu_custom_call" | custom-call | flops 8589934592 | bytes 4194304 | tf_op jit(solution)/shard_map/attend_local/pallas_call | solution.py:142
  45.4 4.5 %collective-permute-start.6 = (bf16[2,512,768]{2,1,0:T(8,128)(2,1)}, bf16[2,512,768]{2,1,0:T(8,128)(2,1)}, u32[]{:S(2)}, u32[]{:S(2)}) collective-permute-start(bf16[2,512,768]{2,1,0:T(8,128)(2,1)} %slice.70), channel_id=1, source_target_pairs={{1,0},{2,1},{3,2},{4,3},{5,4},{6,5},{7,6},{8,7},{9,8},{10,9},{11,1... | collective-permute-start | bytes 4718600 | tf_op jit(solution)/shard_map/ppermute | solution.py:245
  50.0 8.4 %attend_halo.2 = bf16[1024,768]{1,0:T(8,128)(2,1)} custom-call(s32[4,6]{1,0:T(4,128)S(1)} %stack.2.bounds, bf16[512,1536]{1,0:T(8,128)(2,1)S(1)} %copy-done.6, bf16[512,1536]{1,0:T(8,128)(2,1)S(1)} %copy-done.6, bf16[2,512,768]{2,1,0:T(8,128)(2,1)} %collective-permute-done.before_ref, bf16[2,512,768]{2,1,0:T(8,128)(2,1)} %collective-permute-done.1.after_ref, ...), custom_call_target="tpu_custom_call" | custom-call | flops 17179869184 | bytes 4194304 | tf_op jit(solution)/shard_map/attend_halo/pallas_call | solution.py:169
  58.4 7.8 %all-to-all-start = ((bf16[16,64,768]{2,1,0:T(8,128)(2,1)}), bf16[16,64,768]{2,1,0:T(8,128)(2,1)}, u32[]{:S(2)}, u32[]{:S(2)}) async-start(bf16[16,64,768]{2,1,0:T(8,128)(2,1)} %bitcast.13), calls=%async_computation | async-start | bytes 3145728 | tf_op jit(solution)/shard_map/all_to_all | solution.py:298
  67.6 7.8 %collective-permute-done.6.after_ref = bf16[2,512,768]{2,1,0:T(8,128)(2,1)} collective-permute-done((bf16[2,512,768]{2,1,0:T(8,128)(2,1)}, bf16[2,512,768]{2,1,0:T(8,128)(2,1)}, u32[]{:S(2)}, u32[]{:S(2)}) %collective-permute-start.6) | collective-permute-done | bytes 1572896 | tf_op jit(solution)/shard_map/ppermute | solution.py:245
  76.7 8.4 %attend_halo.3 = bf16[1024,768]{1,0:T(8,128)(2,1)} custom-call(s32[4,6]{1,0:T(4,128)S(1)} %stack.2.bounds, bf16[512,1536]{1,0:T(8,128)(2,1)S(1)} %copy-done.7, bf16[512,1536]{1,0:T(8,128)(2,1)S(1)} %copy-done.7, bf16[2,512,768]{2,1,0:T(8,128)(2,1)} %collective-permute-done.5.before_ref, bf16[2,512,768]{2,1,0:T(8,128)(2,1)} %collective-permute-done.6.after_ref, ...), custom_call_target="tpu_custom_call" | custom-call | flops 17179869184 | bytes 4194304 | tf_op jit(solution)/shard_map/attend_halo/pallas_call | solution.py:169
  85.1 16.1 %all-to-all-done = bf16[16,64,768]{2,1,0:T(8,128)(2,1)} async-done(((bf16[16,64,768]{2,1,0:T(8,128)(2,1)}), bf16[16,64,768]{2,1,0:T(8,128)(2,1)}, u32[]{:S(2)}, u32[]{:S(2)}) %all-to-all-start) | async-done | bytes 1572896 | tf_op jit(solution)/shard_map/all_to_all | solution.py:298
  101.2 10.1 %all-to-all-start.2 = ((bf16[16,64,768]{2,1,0:T(8,128)(2,1)}), bf16[16,64,768]{2,1,0:T(8,128)(2,1)}, u32[]{:S(2)}, u32[]{:S(2)}) async-start(bf16[16,64,768]{2,1,0:T(8,128)(2,1)} %bitcast.25), calls=%async_computation.2 | async-start | bytes 3145728 | tf_op jit(solution)/shard_map/all_to_all | solution.py:298
  111.3 2.7 %fusion.32 = bf16[768,512]{1,0:T(8,128)(2,1)S(1)} fusion(bf16[1024,768]{1,0:T(8,128)(2,1)} %bitcast.14, s32[1024]{0:T(1024)S(1)} %eq.76), kind=kOutput, calls=%fused_computation.49 | convolution fusion | flops 806223872 | bytes 2363392 | tf_op jit(solution)/shard_map/sk,sr->kr/dot_general | solution.py:305
  121.0 2.7 %fusion.7 = bf16[2,96,1536]{2,1,0:T(8,128)(2,1)} fusion(f32[2,96,1536]{2,1,0:T(8,128)S(1)} %fusion.22, bf16[512,3072]{1,0:T(8,128)(2,1)} %collective-permute-done.3, bf16[2,2,96,512]{3,2,1,0:T(8,128)(2,1)S(1)} %bitcast.202, s32[]{:T(128)S(6)} %select_n.209), kind=kOutput, calls=%fused_computation.17 | convolution fusion | flops 302579712 | bytes 3538948 | tf_op jit(solution)/shard_map/fbt,td->fbd/dot_general | solution.py:293
  126.3 4.9 %add_add_fusion = f32[512,3072]{1,0:T(8,128)} fusion(f32[512,3072]{1,0:T(8,128)S(1)} %fusion.11, bf16[512,3072]{1,0:T(8,128)(2,1)S(1)} %copy-done.12, bf16[1536,3072]{1,0:T(8,128)(2,1)S(1)} %bitcast.184, bf16[768,512]{1,0:T(8,128)(2,1)S(1)} %fusion.32), kind=kOutput, calls=%fused_computation.1 | convolution fusion | flops 1212678144 | bytes 18481152 | tf_op jit(solution)/shard_map/kr,kd->rd/dot_general | solution.py:383
  131.2 13.2 %collective-permute-done.4 = bf16[2,96,1536]{2,1,0:T(8,128)(2,1)S(1)} collective-permute-done((bf16[2,96,1536]{2,1,0:T(8,128)(2,1)S(1)}, bf16[2,96,1536]{2,1,0:T(8,128)(2,1)S(1)}, u32[]{:S(2)}, u32[]{:S(2)}) %collective-permute-start.4) | collective-permute-done | bytes 589856 | tf_op jit(solution)/shard_map/ppermute | solution.py:232
  147.4 3.0 %collective-permute-start.16 = (bf16[96,1536]{1,0:T(8,128)(2,1)}, bf16[96,1536]{1,0:T(8,128)(2,1)}, u32[]{:S(2)}, u32[]{:S(2)}) collective-permute-start(bf16[96,1536]{1,0:T(8,128)(2,1)} %get-tuple-element.66), channel_id=1, source_target_pairs={{4,0},{5,1},{6,2},{7,3},{8,12},{9,13},{10,14},{11,15},{20,16},{21,... | collective-permute-start | bytes 884744 | tf_op jit(solution)/shard_map/ppermute | solution.py:372
  170.4 4.7 %collective-permute-start.21 = (bf16[96,1536]{1,0:T(8,128)(2,1)S(1)}, bf16[96,1536]{1,0:T(8,128)(2,1)S(1)}, u32[]{:S(2)}, u32[]{:S(2)}) collective-permute-start(bf16[96,1536]{1,0:T(8,128)(2,1)S(1)} %get-tuple-element.68), channel_id=1, source_target_pairs={{4,12},{5,13},{6,14},{7,15},{8,0},{9,1},{10,2},{11,3},{20,28},{21,... | collective-permute-start | bytes 884744 | tf_op jit(solution)/shard_map/ppermute | solution.py:372
  177.9 6.1 %collective-permute-done.8 = bf16[2,96,1536]{2,1,0:T(8,128)(2,1)S(1)} collective-permute-done((bf16[2,96,1536]{2,1,0:T(8,128)(2,1)S(1)}, bf16[2,96,1536]{2,1,0:T(8,128)(2,1)S(1)}, u32[]{:S(2)}, u32[]{:S(2)}) %collective-permute-start.8) | collective-permute-done | bytes 589856 | tf_op jit(solution)/shard_map/ppermute | solution.py:232
  189.8 6.1 %collective-permute-done.12 = bf16[2,96,1536]{2,1,0:T(8,128)(2,1)S(1)} collective-permute-done((bf16[2,96,1536]{2,1,0:T(8,128)(2,1)S(1)}, bf16[2,96,1536]{2,1,0:T(8,128)(2,1)S(1)}, u32[]{:S(2)}, u32[]{:S(2)}) %collective-permute-start.12) | collective-permute-done | bytes 589856 | tf_op jit(solution)/shard_map/ppermute | solution.py:232
  200.9 2.7 %fusion = f32[512,3072]{1,0:T(8,128)S(1)} fusion(bf16[768,512]{1,0:T(8,128)(2,1)S(1)} %fusion.33, bf16[1536,3072]{1,0:T(8,128)(2,1)S(1)} %bitcast.186), kind=kOutput, calls=%fused_computation.2 | convolution fusion | flops 2415919104 | bytes 11796480 | tf_op jit(solution)/shard_map/kr,kd->rd/dot_general | solution.py:383
  206.5 2.7 %collective-permute-start.11 = (bf16[96,1536]{1,0:T(8,128)(2,1)S(1)}, bf16[96,1536]{1,0:T(8,128)(2,1)S(1)}, u32[]{:S(2)}, u32[]{:S(2)}) collective-permute-start(bf16[96,1536]{1,0:T(8,128)(2,1)S(1)} %fusion.45), channel_id=1, source_target_pairs={{4,8},{5,9},{6,10},{7,11},{8,4},{9,5},{10,6},{11,7},{20,24},{21,25... | collective-permute-start | bytes 884744 | tf_op jit(solution)/shard_map/ppermute | solution.py:342
  211.1 2.7 %collective-permute-start.15 = (bf16[96,1536]{1,0:T(8,128)(2,1)S(1)}, bf16[96,1536]{1,0:T(8,128)(2,1)S(1)}, u32[]{:S(2)}, u32[]{:S(2)}) collective-permute-start(bf16[96,1536]{1,0:T(8,128)(2,1)S(1)} %fusion.44), channel_id=1, source_target_pairs={{4,8},{5,9},{6,10},{7,11},{8,4},{9,5},{10,6},{11,7},{20,24},{21,25... | collective-permute-start | bytes 884744 | tf_op jit(solution)/shard_map/ppermute | solution.py:342
  213.9 4.5 %collective-permute-done.11 = bf16[96,1536]{1,0:T(8,128)(2,1)S(1)} collective-permute-done((bf16[96,1536]{1,0:T(8,128)(2,1)S(1)}, bf16[96,1536]{1,0:T(8,128)(2,1)S(1)}, u32[]{:S(2)}, u32[]{:S(2)}) %collective-permute-start.11) | collective-permute-done | bytes 294944 | tf_op jit(solution)/shard_map/ppermute | solution.py:342
  218.5 4.6 %collective-permute-done.15 = bf16[96,1536]{1,0:T(8,128)(2,1)S(1)} collective-permute-done((bf16[96,1536]{1,0:T(8,128)(2,1)S(1)}, bf16[96,1536]{1,0:T(8,128)(2,1)S(1)}, u32[]{:S(2)}, u32[]{:S(2)}) %collective-permute-start.15) | collective-permute-done | bytes 294944 | tf_op jit(solution)/shard_map/ppermute | solution.py:342
  (160 shorter events, 73.5 us)
Async XLA Ops:
  3.5 40.0 %collective-permute-start = (bf16[2,512,768]{2,1,0:T(8,128)(2,1)}, bf16[2,512,768]{2,1,0:T(8,128)(2,1)}, u32[]{:S(2)}, u32[]{:S(2)}) collective-permute-start(bf16[2,512,768]{2,1,0:T(8,128)(2,1)} %pad_maximum_fusion), channel_id=1, source_target_pairs={{0,1},{1,2},{2,3},{3,4},{4,5},{5,6},{6,7},{7,8},{8,9},{9,10},{10,1... | collective-permute-start | bytes 4718600 | tf_op jit(solution)/shard_map/ppermute | solution.py:244
  5.5 38.0 %collective-permute-start.1 = (bf16[2,512,768]{2,1,0:T(8,128)(2,1)}, bf16[2,512,768]{2,1,0:T(8,128)(2,1)}, u32[]{:S(2)}, u32[]{:S(2)}) collective-permute-start(bf16[2,512,768]{2,1,0:T(8,128)(2,1)} %pad_maximum_fusion), channel_id=1, source_target_pairs={{1,0},{2,1},{3,2},{4,3},{5,4},{6,5},{7,6},{8,7},{9,8},{10,9},{11,1... | collective-permute-start | bytes 4718600 | tf_op jit(solution)/shard_map/ppermute | solution.py:245
  13.0 45.4 %all-to-all-start.1 = ((s32[16,1,64]{2,1,0:T(1,128)}), s32[16,1,64]{2,1,0:T(1,128)S(1)}, u32[]{:S(2)}, u32[]{:S(2)}) async-start(s32[16,1,64]{2,1,0:T(1,128)} %select_n.204), calls=%async_computation.1 | async-start | bytes 16384 | tf_op jit(solution)/shard_map/all_to_all | solution.py:264
  43.5 24.0 %collective-permute-start.5 = (bf16[2,512,768]{2,1,0:T(8,128)(2,1)}, bf16[2,512,768]{2,1,0:T(8,128)(2,1)}, u32[]{:S(2)}, u32[]{:S(2)}) collective-permute-start(bf16[2,512,768]{2,1,0:T(8,128)(2,1)} %slice.70), channel_id=1, source_target_pairs={{0,1},{1,2},{2,3},{3,4},{4,5},{5,6},{6,7},{7,8},{8,9},{9,10},{10,1... | collective-permute-start | bytes 4718600 | tf_op jit(solution)/shard_map/ppermute | solution.py:244
  45.4 29.9 %collective-permute-start.6 = (bf16[2,512,768]{2,1,0:T(8,128)(2,1)}, bf16[2,512,768]{2,1,0:T(8,128)(2,1)}, u32[]{:S(2)}, u32[]{:S(2)}) collective-permute-start(bf16[2,512,768]{2,1,0:T(8,128)(2,1)} %slice.70), channel_id=1, source_target_pairs={{1,0},{2,1},{3,2},{4,3},{5,4},{6,5},{7,6},{8,7},{9,8},{10,9},{11,1... | collective-permute-start | bytes 4718600 | tf_op jit(solution)/shard_map/ppermute | solution.py:245
  58.4 42.8 %all-to-all-start = ((bf16[16,64,768]{2,1,0:T(8,128)(2,1)}), bf16[16,64,768]{2,1,0:T(8,128)(2,1)}, u32[]{:S(2)}, u32[]{:S(2)}) async-start(bf16[16,64,768]{2,1,0:T(8,128)(2,1)} %bitcast.13), calls=%async_computation | async-start | bytes 3145728 | tf_op jit(solution)/shard_map/all_to_all | solution.py:298
  66.2 51.4 %collective-permute-start.3 = (bf16[512,3072]{1,0:T(8,128)(2,1)}, bf16[512,3072]{1,0:T(8,128)(2,1)}, u32[]{:S(2)}, u32[]{:S(2)}) collective-permute-start(bf16[512,3072]{1,0:T(8,128)(2,1)} %param.15), channel_id=1, source_target_pairs={{0,1},{1,0},{2,3},{3,2},{4,5},{5,4},{6,7},{7,6},{8,9},{9,8},{10,11... | collective-permute-start | bytes 9437192 | tf_op jit(solution)/shard_map/ppermute | solution.py:232
  101.2 53.4 %all-to-all-start.2 = ((bf16[16,64,768]{2,1,0:T(8,128)(2,1)}), bf16[16,64,768]{2,1,0:T(8,128)(2,1)}, u32[]{:S(2)}, u32[]{:S(2)}) async-start(bf16[16,64,768]{2,1,0:T(8,128)(2,1)} %bitcast.25), calls=%async_computation.2 | async-start | bytes 3145728 | tf_op jit(solution)/shard_map/all_to_all | solution.py:298
  119.6 24.9 %collective-permute-start.4 = (bf16[2,96,1536]{2,1,0:T(8,128)(2,1)S(1)}, bf16[2,96,1536]{2,1,0:T(8,128)(2,1)S(1)}, u32[]{:S(2)}, u32[]{:S(2)}) collective-permute-start(bf16[2,96,1536]{2,1,0:T(8,128)(2,1)S(1)} %fusion.6), channel_id=1, source_target_pairs={{0,2},{1,3},{2,0},{3,1},{4,6},{5,7},{6,4},{7,5},{8,10},{9,11},{10,... | collective-permute-start | bytes 1769480 | tf_op jit(solution)/shard_map/ppermute | solution.py:232
  123.7 35.2 %collective-permute-start.19 = (bf16[2,96,1536]{2,1,0:T(8,128)(2,1)}, bf16[2,96,1536]{2,1,0:T(8,128)(2,1)}, u32[]{:S(2)}, u32[]{:S(2)}) collective-permute-start(bf16[2,96,1536]{2,1,0:T(8,128)(2,1)} %fusion.7), channel_id=1, source_target_pairs={{0,2},{1,3},{2,0},{3,1},{4,6},{5,7},{6,4},{7,5},{8,10},{9,11},{10,... | collective-permute-start | bytes 1769480 | tf_op jit(solution)/shard_map/ppermute | solution.py:232
  147.4 23.0 %collective-permute-start.16 = (bf16[96,1536]{1,0:T(8,128)(2,1)}, bf16[96,1536]{1,0:T(8,128)(2,1)}, u32[]{:S(2)}, u32[]{:S(2)}) collective-permute-start(bf16[96,1536]{1,0:T(8,128)(2,1)} %get-tuple-element.66), channel_id=1, source_target_pairs={{4,0},{5,1},{6,2},{7,3},{8,12},{9,13},{10,14},{11,15},{20,16},{21,... | collective-permute-start | bytes 884744 | tf_op jit(solution)/shard_map/ppermute | solution.py:372
  150.4 24.7 %collective-permute-start.17 = (bf16[96,1536]{1,0:T(8,128)(2,1)}, bf16[96,1536]{1,0:T(8,128)(2,1)}, u32[]{:S(2)}, u32[]{:S(2)}) collective-permute-start(bf16[96,1536]{1,0:T(8,128)(2,1)} %get-tuple-element.65), channel_id=1, source_target_pairs={{4,12},{5,13},{6,14},{7,15},{8,0},{9,1},{10,2},{11,3},{20,28},{21,... | collective-permute-start | bytes 884744 | tf_op jit(solution)/shard_map/ppermute | solution.py:372
  152.4 23.7 %collective-permute-start.18 = (bf16[96,1536]{1,0:T(8,128)(2,1)}, bf16[96,1536]{1,0:T(8,128)(2,1)}, u32[]{:S(2)}, u32[]{:S(2)}) collective-permute-start(bf16[96,1536]{1,0:T(8,128)(2,1)} %get-tuple-element.64), channel_id=1, source_target_pairs={{0,12},{1,13},{2,14},{3,15},{12,0},{13,1},{14,2},{15,3},{16,28},{1... | collective-permute-start | bytes 884744 | tf_op jit(solution)/shard_map/ppermute | solution.py:372
  161.7 25.4 %collective-permute-start.20 = (bf16[96,1536]{1,0:T(8,128)(2,1)S(1)}, bf16[96,1536]{1,0:T(8,128)(2,1)S(1)}, u32[]{:S(2)}, u32[]{:S(2)}) collective-permute-start(bf16[96,1536]{1,0:T(8,128)(2,1)S(1)} %get-tuple-element.69), channel_id=1, source_target_pairs={{4,0},{5,1},{6,2},{7,3},{8,12},{9,13},{10,14},{11,15},{20,16},{21,... | collective-permute-start | bytes 884744 | tf_op jit(solution)/shard_map/ppermute | solution.py:372
  167.7 16.2 %collective-permute-start.8 = (bf16[2,96,1536]{2,1,0:T(8,128)(2,1)S(1)}, bf16[2,96,1536]{2,1,0:T(8,128)(2,1)S(1)}, u32[]{:S(2)}, u32[]{:S(2)}) collective-permute-start(bf16[2,96,1536]{2,1,0:T(8,128)(2,1)S(1)} %fusion.8), channel_id=1, source_target_pairs={{0,2},{1,3},{2,0},{3,1},{4,6},{5,7},{6,4},{7,5},{8,10},{9,11},{10,... | collective-permute-start | bytes 1769480 | tf_op jit(solution)/shard_map/ppermute | solution.py:232
  170.4 16.8 %collective-permute-start.21 = (bf16[96,1536]{1,0:T(8,128)(2,1)S(1)}, bf16[96,1536]{1,0:T(8,128)(2,1)S(1)}, u32[]{:S(2)}, u32[]{:S(2)}) collective-permute-start(bf16[96,1536]{1,0:T(8,128)(2,1)S(1)} %get-tuple-element.68), channel_id=1, source_target_pairs={{4,12},{5,13},{6,14},{7,15},{8,0},{9,1},{10,2},{11,3},{20,28},{21,... | collective-permute-start | bytes 884744 | tf_op jit(solution)/shard_map/ppermute | solution.py:372
  175.2 12.0 %collective-permute-start.22 = (bf16[96,1536]{1,0:T(8,128)(2,1)S(1)}, bf16[96,1536]{1,0:T(8,128)(2,1)S(1)}, u32[]{:S(2)}, u32[]{:S(2)}) collective-permute-start(bf16[96,1536]{1,0:T(8,128)(2,1)S(1)} %get-tuple-element.67), channel_id=1, source_target_pairs={{0,12},{1,13},{2,14},{3,15},{12,0},{13,1},{14,2},{15,3},{16,28},{1... | collective-permute-start | bytes 884744 | tf_op jit(solution)/shard_map/ppermute | solution.py:372
  176.1 19.8 %collective-permute-start.12 = (bf16[2,96,1536]{2,1,0:T(8,128)(2,1)S(1)}, bf16[2,96,1536]{2,1,0:T(8,128)(2,1)S(1)}, u32[]{:S(2)}, u32[]{:S(2)}) collective-permute-start(bf16[2,96,1536]{2,1,0:T(8,128)(2,1)S(1)} %fusion.9), channel_id=1, source_target_pairs={{0,2},{1,3},{2,0},{3,1},{4,6},{5,7},{6,4},{7,5},{8,10},{9,11},{10,... | collective-permute-start | bytes 1769480 | tf_op jit(solution)/shard_map/ppermute | solution.py:232
  187.2 19.2 %collective-permute-start.10 = (bf16[96,1536]{1,0:T(8,128)(2,1)S(1)}, bf16[96,1536]{1,0:T(8,128)(2,1)S(1)}, u32[]{:S(2)}, u32[]{:S(2)}) collective-permute-start(bf16[96,1536]{1,0:T(8,128)(2,1)S(1)} %get-tuple-element.71), channel_id=1, source_target_pairs={{0,4},{1,5},{2,6},{3,7},{12,8},{13,9},{14,10},{15,11},{16,20},{17,... | collective-permute-start | bytes 884744 | tf_op jit(solution)/shard_map/ppermute | solution.py:342
  188.5 25.3 %collective-permute-start.9 = (bf16[96,1536]{1,0:T(8,128)(2,1)S(1)}, bf16[96,1536]{1,0:T(8,128)(2,1)S(1)}, u32[]{:S(2)}, u32[]{:S(2)}) collective-permute-start(bf16[96,1536]{1,0:T(8,128)(2,1)S(1)} %get-tuple-element.70), channel_id=1, source_target_pairs={{0,4},{1,5},{2,6},{3,7},{12,8},{13,9},{14,10},{15,11},{16,20},{17,... | collective-permute-start | bytes 884744 | tf_op jit(solution)/shard_map/ppermute | solution.py:342
  197.9 12.2 %collective-permute-start.14 = (bf16[96,1536]{1,0:T(8,128)(2,1)S(1)}, bf16[96,1536]{1,0:T(8,128)(2,1)}, u32[]{:S(2)}, u32[]{:S(2)}) collective-permute-start(bf16[96,1536]{1,0:T(8,128)(2,1)S(1)} %get-tuple-element.73), channel_id=1, source_target_pairs={{0,4},{1,5},{2,6},{3,7},{12,8},{13,9},{14,10},{15,11},{16,20},{17,... | collective-permute-start | bytes 884744 | tf_op jit(solution)/shard_map/ppermute | solution.py:342
  199.5 19.0 %collective-permute-start.13 = (bf16[96,1536]{1,0:T(8,128)(2,1)S(1)}, bf16[96,1536]{1,0:T(8,128)(2,1)S(1)}, u32[]{:S(2)}, u32[]{:S(2)}) collective-permute-start(bf16[96,1536]{1,0:T(8,128)(2,1)S(1)} %get-tuple-element.72), channel_id=1, source_target_pairs={{0,4},{1,5},{2,6},{3,7},{12,8},{13,9},{14,10},{15,11},{16,20},{17,... | collective-permute-start | bytes 884744 | tf_op jit(solution)/shard_map/ppermute | solution.py:342
  206.5 11.8 %collective-permute-start.11 = (bf16[96,1536]{1,0:T(8,128)(2,1)S(1)}, bf16[96,1536]{1,0:T(8,128)(2,1)S(1)}, u32[]{:S(2)}, u32[]{:S(2)}) collective-permute-start(bf16[96,1536]{1,0:T(8,128)(2,1)S(1)} %fusion.45), channel_id=1, source_target_pairs={{4,8},{5,9},{6,10},{7,11},{8,4},{9,5},{10,6},{11,7},{20,24},{21,25... | collective-permute-start | bytes 884744 | tf_op jit(solution)/shard_map/ppermute | solution.py:342
  211.1 11.9 %collective-permute-start.15 = (bf16[96,1536]{1,0:T(8,128)(2,1)S(1)}, bf16[96,1536]{1,0:T(8,128)(2,1)S(1)}, u32[]{:S(2)}, u32[]{:S(2)}) collective-permute-start(bf16[96,1536]{1,0:T(8,128)(2,1)S(1)} %fusion.44), channel_id=1, source_target_pairs={{4,8},{5,9},{6,10},{7,11},{8,4},{9,5},{10,6},{11,7},{20,24},{21,25... | collective-permute-start | bytes 884744 | tf_op jit(solution)/shard_map/ppermute | solution.py:342
  (28 other events, 301.7 us)
